TPU v7x, 256 devices: a whole 4x4x8 slice. The times are simulated.
256 devices in a mesh: tm: 64 (over y_hi, z, x), head: 4 (over y_lo, core).
Axes of the slice: x: 4, y: 4 (y_hi: 2, y_lo: 2; y = y_hi * 2 + y_lo), z: 8, core: 2. Of those that a mesh axis runs over, the one named last changes fastest.
Arguments:
- query: bfloat16 [32768, 2560], P(('tm', 'head')), may hold values from -5 to 5, as said below
- keys: bfloat16 [32768, 2560], P(('tm', 'head')), may hold values from -5 to 5, as said below
- values: bfloat16 [32768, 2560], P(('tm', 'head')), may hold values from -6 to 6
- grad_out: bfloat16 [32768, 2560], P(('tm', 'head')), may hold values from -6 to 6
- tile_pattern: int32 [3, 4, 3], replicated, may hold values from 0 to 3, as said below
- window: int32 [64], replicated, may hold values from 1 to 3
Outputs:
- attended: bfloat16 [32768, 2560], P(('tm', 'head'))
- grad_query: bfloat16 [32768, 2560], P(('tm', 'head'))
- grad_keys: bfloat16 [32768, 2560], P(('tm', 'head'))
- grad_values: bfloat16 [32768, 2560], P(('tm', 'head'))
Inputs may be any that keep to these rules, and one draw needn't show every extreme that they name: `query`: queries of the attention. `keys`: keys of the attention. `tile_pattern`: entry [l, q, 0] is q; the 3 entries of each row are distinct.
All inputs are finite; a program needn't handle non-finite values.
Results may differ from a plain program's by a relative error of at most 0.0091.
Values may be sent and summed in bfloat16 or wider, within the bound.
A program may use at most 128 MiB of HBM per device.

v0:
```python
from functools import partial
import math

import jax
import jax.numpy as jnp
from jax import lax
from jax.sharding import PartitionSpec as P

HD = 128
QT = 4
SEL = 3
W = 3


NEG = -1e30


def shifted(block, axis, distance):
    devices = range(lax.axis_size(axis))
    route = [(i - distance, i) for i in devices if i - distance in devices]
    return lax.ppermute(block, axis, route)


def to_heads(array, heads_local, tile_len):
    return jnp.transpose(array.reshape(QT, tile_len, heads_local, HD), (2, 0, 1, 3))


def tile_pass(q_all, g_all, keys_all, vals_all, live_cols, carry, inputs):
    acc_k, acc_v = carry
    index, chosen = inputs
    heads_local = q_all.shape[0]
    tile_len = q_all.shape[2]
    count = W * SEL * tile_len
    q_head = lax.dynamic_index_in_dim(q_all, index, 1, False)
    g_head = lax.dynamic_index_in_dim(g_all, index, 1, False)
    k_sel = jnp.concatenate([jnp.take(keys_all[lag], chosen[lag], axis=1) for lag in range(W)], 1)
    v_sel = jnp.concatenate([jnp.take(vals_all[lag], chosen[lag], axis=1) for lag in range(W)], 1)
    k_sel = k_sel.reshape(heads_local, count, HD)
    v_sel = v_sel.reshape(heads_local, count, HD)
    scale = 1.0 / math.sqrt(HD)
    scores = jnp.einsum("had,hbd->hab", q_head, k_sel, preferred_element_type=jnp.float32) * scale
    scores = jnp.where(live_cols, scores, NEG)
    top = jnp.max(scores, -1, keepdims=True)
    expo = jnp.exp(scores - top)
    prob = expo / jnp.sum(expo, -1, keepdims=True)
    prob_b = prob.astype(jnp.bfloat16)
    output = jnp.einsum("hab,hbd->had", prob_b, v_sel, preferred_element_type=jnp.float32)
    delta = jnp.sum(g_head.astype(jnp.float32) * output, -1, keepdims=True)
    dprob = jnp.einsum("had,hbd->hab", g_head, v_sel, preferred_element_type=jnp.float32)
    dscore = (prob * (dprob - delta) * scale).astype(jnp.bfloat16)
    dquery = jnp.einsum("hab,hbd->had", dscore, k_sel, preferred_element_type=jnp.float32)
    dkeys = jnp.einsum("hab,had->hbd", dscore, q_head, preferred_element_type=jnp.float32)
    dvals = jnp.einsum("hab,had->hbd", prob_b, g_head, preferred_element_type=jnp.float32)
    dkeys = dkeys.reshape(heads_local, W, SEL, tile_len, HD)
    dvals = dvals.reshape(heads_local, W, SEL, tile_len, HD)
    onehot = (chosen[:, :, None] == jnp.arange(QT, dtype=jnp.int32)[None, None, :]).astype(
        jnp.float32
    )
    highest = lax.Precision.HIGHEST
    acc_k = acc_k + jnp.einsum("hwstd,wsk->whktd", dkeys, onehot, precision=highest)
    acc_v = acc_v + jnp.einsum("hwstd,wsk->whktd", dvals, onehot, precision=highest)
    return ((acc_k, acc_v), (output.astype(jnp.bfloat16), dquery.astype(jnp.bfloat16)))


def shards(query, keys, values, grad_out, tile_pattern, window):
    q_loc, k_loc, v_loc, g_loc = (
        lax.all_to_all(query, "head", split_axis=1, concat_axis=0, tiled=True),
        lax.all_to_all(keys, "head", split_axis=1, concat_axis=0, tiled=True),
        lax.all_to_all(values, "head", split_axis=1, concat_axis=0, tiled=True),
        lax.all_to_all(grad_out, "head", split_axis=1, concat_axis=0, tiled=True),
    )
    frame_len = q_loc.shape[0]
    width = q_loc.shape[1]
    heads_local = width // HD
    tile_len = frame_len // QT
    frame = lax.axis_index("tm")
    q_all = to_heads(q_loc, heads_local, tile_len)
    g_all = to_heads(g_loc, heads_local, tile_len)
    paired = jnp.stack(
        (to_heads(k_loc, heads_local, tile_len), to_heads(v_loc, heads_local, tile_len))
    )
    earlier = [paired]
    for lag in range(1, W):
        earlier.append(shifted(paired, "tm", lag))
    keys_all = [piece[0] for piece in earlier]
    vals_all = [piece[1] for piece in earlier]
    lags = jnp.arange(W, dtype=jnp.int32)
    limit = lax.dynamic_index_in_dim(window, frame, 0, False)
    live = (lags <= frame) & (lags < limit)
    live_cols = jnp.repeat(live, SEL * tile_len)
    sel_tiles = jnp.transpose(tile_pattern, (1, 0, 2))
    zeros = jnp.zeros((W, heads_local, QT, tile_len, HD), jnp.float32)
    stepper = partial(tile_pass, q_all, g_all, keys_all, vals_all, live_cols)
    tile_ids = jnp.arange(QT, dtype=jnp.int32)
    (acc_k, acc_v), (out_tiles, dq_tiles) = lax.scan(stepper, (zeros, zeros), (tile_ids, sel_tiles))
    grad_pairs = jnp.stack((acc_k, acc_v), 1)
    pending = grad_pairs[W - 1].astype(jnp.bfloat16)
    total = grad_pairs[0]
    for lag in range(W - 1, 0, -1):
        moved = shifted(pending, "tm", -1)
        if lag > 1:
            pending = (grad_pairs[lag - 1] + moved.astype(jnp.float32)).astype(jnp.bfloat16)
        else:
            total = total + moved.astype(jnp.float32)
    out_loc = jnp.transpose(out_tiles, (0, 2, 1, 3)).reshape(frame_len, width)
    dq_loc = jnp.transpose(dq_tiles, (0, 2, 1, 3)).reshape(frame_len, width)
    dk_loc = jnp.transpose(total[0], (1, 2, 0, 3)).reshape(frame_len, width).astype(jnp.bfloat16)
    dv_loc = jnp.transpose(total[1], (1, 2, 0, 3)).reshape(frame_len, width).astype(jnp.bfloat16)
    attended, grad_query, grad_keys, grad_values = (
        lax.all_to_all(out_loc, "head", split_axis=0, concat_axis=1, tiled=True),
        lax.all_to_all(dq_loc, "head", split_axis=0, concat_axis=1, tiled=True),
        lax.all_to_all(dk_loc, "head", split_axis=0, concat_axis=1, tiled=True),
        lax.all_to_all(dv_loc, "head", split_axis=0, concat_axis=1, tiled=True),
    )
    return (attended, grad_query, grad_keys, grad_values)


def solution(mesh):
    placed = (
        P(("tm", "head"), None),
        P(("tm", "head"), None),
        P(("tm", "head"), None),
        P(("tm", "head"), None),
        P(),
        P(),
    )
    return jax.shard_map(
        shards,
        mesh=mesh,
        in_specs=placed,
        out_specs=(
            P(("tm", "head"), None),
            P(("tm", "head"), None),
            P(("tm", "head"), None),
            P(("tm", "head"), None),
        ),
        check_vma=False,
    )
```

profile of v0, /device:TPU:246, one launch (start us, length us, event | category | flops | bytes accessed | tf_op | source)
XLA Modules:
  0.0 443.3 jit_solution(4937883007304398034)
XLA Ops:
  2.9 3.5 all-to-all-start.1
  6.7 9.8 %all-to-all-done.1 = bf16[128,4,640]{0,2,1:T(8,128)(2,1)S(1)} async-done(((bf16[128,4,640]{0,2,1:T(8,128)(2,1)}), bf16[128,4,640]{0,2,1:T(8,128)(2,1)S(1)}, u32[]{:S(2)}, u32[]{:S(2)}) %all-to-all-start.1) | async-done | bytes 655392 | tf_op jit(solution)/shard_map/all_to_all | solution.py:68
  16.5 12.6 %all_to_all.134 = bf16[128,4,640]{0,2,1:T(8,128)(2,1)S(1)} all-to-all(bf16[128,4,640]{0,2,1:T(8,128)(2,1)S(1)} %bitcast.231), channel_id=1, replica_groups=mesh['tm'=64,'head'=4] {'head'}, dimensions={1} | all-to-all | bytes 1310720 | tf_op jit(solution)/shard_map/all_to_all | solution.py:69
  34.2 4.2 all-to-all-start
  41.5 7.2 %all-to-all-done = bf16[128,4,640]{0,2,1:T(8,128)(2,1)} async-done(((bf16[128,4,640]{0,2,1:T(8,128)(2,1)}), bf16[128,4,640]{0,2,1:T(8,128)(2,1)}, u32[]{:S(2)}, u32[]{:S(2)}) %all-to-all-start) | async-done | bytes 655392 | tf_op jit(solution)/shard_map/all_to_all | solution.py:67
  48.7 3.5 all-to-all-start.3
  52.2 12.2 %collective-permute-done.1 = bf16[2,5,4,128,128]{3,4,1,2,0:T(8,128)(2,1)} collective-permute-done((bf16[2,5,4,128,128]{3,4,1,2,0:T(8,128)(2,1)}, bf16[2,5,4,128,128]{3,4,1,2,0:T(8,128)(2,1)}, u32[]{:S(2)}, u32[]{:S(2)}) %collective-permute-start.1) | collective-permute-done | bytes 1310752 | tf_op jit(solution)/shard_map/ppermute | solution.py:21
  69.9 21.3 %collective-permute-done = bf16[2,5,4,128,128]{3,4,1,2,0:T(8,128)(2,1)} collective-permute-done((bf16[2,5,4,128,128]{3,4,1,2,0:T(8,128)(2,1)}, bf16[2,5,4,128,128]{3,4,1,2,0:T(8,128)(2,1)}, u32[]{:S(2)}, u32[]{:S(2)}) %collective-permute-start) | collective-permute-done | bytes 1310752 | tf_op jit(solution)/shard_map/ppermute | solution.py:21
  96.7 210.7 %while.17 = (s32[]{:T(128)}, f32[3,5,4,128,128]{4,2,3,1,0:T(4,128)}, f32[3,5,4,128,128]{4,2,3,1,0:T(4,128)}, bf16[4,5,128,128]{2,3,1,0:T(8,128)(2,1)}, bf16[4,5,...) while((s32[]{:T(128)}, ...), condition=%wide.region_4.6_spmd.clone, body=%wide.region_0.5_spmd.clone.sunk | while | flops 1220120320 | bytes 180746352 | solution.py:95
  109.5 3.9 fusion.107
  126.1 8.8 %bitcast_add_fusion.5 = f32[3,5,4,128,128]{4,2,3,1,0:T(4,128)S(1)} fusion(f32[3,5,4,128,128]{4,2,3,1,0:T(4,128)S(1)} %copy-done, f32[5,3,3,128,128]{4,3,2,1,0:T(8,128)S(1)} %bitcast.210, pred[]{:T(512)S(6)} %compare.3, s32[3,3]{1,0:T(4,128)S(1)} %fusion.111), kind=kOutput, calls=%fused_computation.9.clone.1 | convolution fusion | flops 37355556 | bytes 10813477 | tf_op jit(solution)/shard_map/while/body/eval_jaxpr/hwstd,wsk->whktd/dot_general | solution.py:61
  138.6 8.9 %bitcast_add_fusion.4 = f32[3,5,4,128,128]{4,2,3,1,0:T(4,128)S(1)} fusion(f32[3,5,4,128,128]{4,2,3,1,0:T(4,128)S(1)} %copy-done.2, f32[5,3,3,128,128]{4,3,2,1,0:T(8,128)S(1)} %bitcast.209, pred[]{:T(512)S(6)} %compare.3, s32[3,3]{1,0:T(4,128)S(1)} %fusion.111), kind=kOutput, calls=%fused_computation.10.clone.1 | convolution fusion | flops 37355556 | bytes 10813477 | tf_op jit(solution)/shard_map/while/body/eval_jaxpr/hwstd,wsk->whktd/dot_general | solution.py:60
  162.2 3.9 fusion.107
  178.8 8.8 %bitcast_add_fusion.5 = f32[3,5,4,128,128]{4,2,3,1,0:T(4,128)S(1)} fusion(f32[3,5,4,128,128]{4,2,3,1,0:T(4,128)S(1)} %copy-done, f32[5,3,3,128,128]{4,3,2,1,0:T(8,128)S(1)} %bitcast.210, pred[]{:T(512)S(6)} %compare.3, s32[3,3]{1,0:T(4,128)S(1)} %fusion.111), kind=kOutput, calls=%fused_computation.9.clone.1 | convolution fusion | flops 37355556 | bytes 10813477 | tf_op jit(solution)/shard_map/while/body/eval_jaxpr/hwstd,wsk->whktd/dot_general | solution.py:61
  191.3 8.8 %bitcast_add_fusion.4 = f32[3,5,4,128,128]{4,2,3,1,0:T(4,128)S(1)} fusion(f32[3,5,4,128,128]{4,2,3,1,0:T(4,128)S(1)} %copy-done.2, f32[5,3,3,128,128]{4,3,2,1,0:T(8,128)S(1)} %bitcast.209, pred[]{:T(512)S(6)} %compare.3, s32[3,3]{1,0:T(4,128)S(1)} %fusion.111), kind=kOutput, calls=%fused_computation.10.clone.1 | convolution fusion | flops 37355556 | bytes 10813477 | tf_op jit(solution)/shard_map/while/body/eval_jaxpr/hwstd,wsk->whktd/dot_general | solution.py:60
  214.9 3.9 fusion.107
  231.5 8.8 %bitcast_add_fusion.5 = f32[3,5,4,128,128]{4,2,3,1,0:T(4,128)S(1)} fusion(f32[3,5,4,128,128]{4,2,3,1,0:T(4,128)S(1)} %copy-done, f32[5,3,3,128,128]{4,3,2,1,0:T(8,128)S(1)} %bitcast.210, pred[]{:T(512)S(6)} %compare.3, s32[3,3]{1,0:T(4,128)S(1)} %fusion.111), kind=kOutput, calls=%fused_computation.9.clone.1 | convolution fusion | flops 37355556 | bytes 10813477 | tf_op jit(solution)/shard_map/while/body/eval_jaxpr/hwstd,wsk->whktd/dot_general | solution.py:61
  244.0 8.8 %bitcast_add_fusion.4 = f32[3,5,4,128,128]{4,2,3,1,0:T(4,128)S(1)} fusion(f32[3,5,4,128,128]{4,2,3,1,0:T(4,128)S(1)} %copy-done.2, f32[5,3,3,128,128]{4,3,2,1,0:T(8,128)S(1)} %bitcast.209, pred[]{:T(512)S(6)} %compare.3, s32[3,3]{1,0:T(4,128)S(1)} %fusion.111), kind=kOutput, calls=%fused_computation.10.clone.1 | convolution fusion | flops 37355556 | bytes 10813477 | tf_op jit(solution)/shard_map/while/body/eval_jaxpr/hwstd,wsk->whktd/dot_general | solution.py:60
  267.5 3.9 fusion.107
  284.2 8.8 %bitcast_add_fusion.5 = f32[3,5,4,128,128]{4,2,3,1,0:T(4,128)S(1)} fusion(f32[3,5,4,128,128]{4,2,3,1,0:T(4,128)S(1)} %copy-done, f32[5,3,3,128,128]{4,3,2,1,0:T(8,128)S(1)} %bitcast.210, pred[]{:T(512)S(6)} %compare.3, s32[3,3]{1,0:T(4,128)S(1)} %fusion.111), kind=kOutput, calls=%fused_computation.9.clone.1 | convolution fusion | flops 37355556 | bytes 10813477 | tf_op jit(solution)/shard_map/while/body/eval_jaxpr/hwstd,wsk->whktd/dot_general | solution.py:61
  296.7 8.8 %bitcast_add_fusion.4 = f32[3,5,4,128,128]{4,2,3,1,0:T(4,128)S(1)} fusion(f32[3,5,4,128,128]{4,2,3,1,0:T(4,128)S(1)} %copy-done.2, f32[5,3,3,128,128]{4,3,2,1,0:T(8,128)S(1)} %bitcast.209, pred[]{:T(512)S(6)} %compare.3, s32[3,3]{1,0:T(4,128)S(1)} %fusion.111), kind=kOutput, calls=%fused_computation.10.clone.1 | convolution fusion | flops 37355556 | bytes 10813477 | tf_op jit(solution)/shard_map/while/body/eval_jaxpr/hwstd,wsk->whktd/dot_general | solution.py:60
  307.4 6.3 %copy.106 = f32[3,5,4,128,128]{3,4,1,2,0:T(8,128)} copy(f32[3,5,4,128,128]{4,2,3,1,0:T(4,128)} %get-tuple-element.92) | data formatting | bytes 7864320 | tf_op jit(solution)/shard_map/while | solution.py:95
  313.7 6.3 %copy.107 = f32[3,5,4,128,128]{3,4,1,2,0:T(8,128)} copy(f32[3,5,4,128,128]{4,2,3,1,0:T(4,128)} %get-tuple-element.93) | data formatting | bytes 7864320 | tf_op jit(solution)/shard_map/while | solution.py:95
  322.0 4.4 collective-permute-start.2
  326.5 28.1 %collective-permute-done.2 = bf16[2,5,4,128,128]{3,4,1,2,0:T(8,128)(2,1)S(1)} collective-permute-done((bf16[2,5,4,128,128]{3,4,1,2,0:T(8,128)(2,1)S(1)}, bf16[2,5,4,128,128]{3,4,1,2,0:T(8,128)(2,1)S(1)}, u32[]{:S(2)}, u32[]{:S(2)}) %collective-permute-start.2) | collective-permute-done | bytes 1310752 | tf_op jit(solution)/shard_map/ppermute | solution.py:21
  356.0 4.5 %collective-permute-start.3 = (bf16[2,5,4,128,128]{3,4,1,2,0:T(8,128)(2,1)}, bf16[2,5,4,128,128]{3,4,1,2,0:T(8,128)(2,1)S(1)}, u32[]{:S(2)}, u32[]{:S(2)}) collective-permute-start(bf16[2,5,4,128,128]{3,4,1,2,0:T(8,128)(2,1)} %fusion.48), channel_id=1, source_target_pairs={{4,0},{8,4},{12,8},{16,12},{20,16},{24,20},{28,24},{32,28},{36,32}... | collective-permute-start | bytes 3932168 | tf_op jit(solution)/shard_map/ppermute | solution.py:21
  360.5 3.5 all-to-all-start.5
  365.1 37.2 %all-to-all-done.5 = bf16[4,128,640]{1,2,0:T(8,128)(2,1)S(1)} async-done(((bf16[4,128,640]{1,2,0:T(8,128)(2,1)}), bf16[4,128,640]{1,2,0:T(8,128)(2,1)S(1)}, u32[]{:S(2)}, u32[]{:S(2)}) %all-to-all-start.5) | async-done | bytes 655392 | tf_op jit(solution)/shard_map/all_to_all | solution.py:111
  402.2 3.5 all-to-all-start.4
  408.9 7.1 %all-to-all-done.4 = bf16[4,128,640]{2,1,0:T(8,128)(2,1)S(1)} async-done(((bf16[4,128,640]{2,1,0:T(8,128)(2,1)}), bf16[4,128,640]{2,1,0:T(8,128)(2,1)S(1)}, u32[]{:S(2)}, u32[]{:S(2)}) %all-to-all-start.4) | async-done | bytes 655392 | tf_op jit(solution)/shard_map/all_to_all | solution.py:110
  415.9 12.6 %all_to_all.135 = bf16[4,128,640]{1,2,0:T(8,128)(2,1)S(1)} all-to-all(bf16[4,128,640]{1,2,0:T(8,128)(2,1)S(1)} %bitcast.226), channel_id=1, replica_groups=mesh['tm'=64,'head'=4] {'head'}, dimensions={0} | all-to-all | bytes 1310720 | tf_op jit(solution)/shard_map/all_to_all | solution.py:112
  435.6 6.6 %all-to-all-done.7 = bf16[4,128,640]{1,2,0:T(8,128)(2,1)S(1)} async-done(((bf16[4,128,640]{1,2,0:T(8,128)(2,1)}), bf16[4,128,640]{1,2,0:T(8,128)(2,1)S(1)}, u32[]{:S(2)}, u32[]{:S(2)}) %all-to-all-start.7) | async-done | bytes 655392 | tf_op jit(solution)/shard_map/all_to_all | solution.py:113
  (296 shorter events, 153.3 us)
Async XLA Ops:
  2.9 13.7 %all-to-all-start.1 = ((bf16[128,4,640]{0,2,1:T(8,128)(2,1)}), bf16[128,4,640]{0,2,1:T(8,128)(2,1)S(1)}, u32[]{:S(2)}, u32[]{:S(2)}) async-start(bf16[128,4,640]{0,2,1:T(8,128)(2,1)} %bitcast.5), calls=%async_computation.1 | async-start | bytes 1310720 | tf_op jit(solution)/shard_map/all_to_all | solution.py:68
  6.7 26.4 %copy-start.17 = (bf16[128,2560]{1,0:T(8,128)(2,1)S(1)}, bf16[128,2560]{1,0:T(8,128)(2,1)}, u32[]{:S(2)}) copy-start(bf16[128,2560]{1,0:T(8,128)(2,1)} %param.10) | copy-start | bytes 1966084
  29.2 9.3 %copy-start.20 = (s32[3,4,3]{2,1,0:T(4,128)S(1)}, s32[3,4,3]{2,1,0:T(4,128)}, u32[]{:S(2)}) copy-start(s32[3,4,3]{2,1,0:T(4,128)} %param.14) | copy-start | bytes 436
  29.2 9.3 %copy-start.18 = (bf16[128,2560]{1,0:T(8,128)(2,1)S(1)}, bf16[128,2560]{1,0:T(8,128)(2,1)}, u32[]{:S(2)}) copy-start(bf16[128,2560]{1,0:T(8,128)(2,1)} %param.13) | copy-start | bytes 1966084
  30.4 34.0 %collective-permute-start.1 = (bf16[2,5,4,128,128]{3,4,1,2,0:T(8,128)(2,1)}, bf16[2,5,4,128,128]{3,4,1,2,0:T(8,128)(2,1)}, u32[]{:S(2)}, u32[]{:S(2)}) collective-permute-start(bf16[2,5,4,128,128]{3,4,1,2,0:T(8,128)(2,1)} %pad_maximum_fusion.3), channel_id=1, source_target_pairs={{0,8},{4,12},{8,16},{12,20},{16,24},{20,28},{24,32},{28,36},{32,40... | collective-permute-start | bytes 3932168 | tf_op jit(solution)/shard_map/ppermute | solution.py:21
  31.8 59.4 %collective-permute-start = (bf16[2,5,4,128,128]{3,4,1,2,0:T(8,128)(2,1)}, bf16[2,5,4,128,128]{3,4,1,2,0:T(8,128)(2,1)}, u32[]{:S(2)}, u32[]{:S(2)}) collective-permute-start(bf16[2,5,4,128,128]{3,4,1,2,0:T(8,128)(2,1)} %pad_maximum_fusion.3), channel_id=1, source_target_pairs={{0,4},{4,8},{8,12},{12,16},{16,20},{20,24},{24,28},{28,32},{32,36}... | collective-permute-start | bytes 3932168 | tf_op jit(solution)/shard_map/ppermute | solution.py:21
  34.2 14.5 %all-to-all-start = ((bf16[128,4,640]{0,2,1:T(8,128)(2,1)}), bf16[128,4,640]{0,2,1:T(8,128)(2,1)}, u32[]{:S(2)}, u32[]{:S(2)}) async-start(bf16[128,4,640]{0,2,1:T(8,128)(2,1)} %bitcast.1), calls=%async_computation | async-start | bytes 1310720 | tf_op jit(solution)/shard_map/all_to_all | solution.py:67
  48.7 48.0 %all-to-all-start.3 = ((bf16[128,4,640]{0,2,1:T(8,128)(2,1)}), bf16[128,4,640]{0,2,1:T(8,128)(2,1)S(1)}, u32[]{:S(2)}, u32[]{:S(2)}) async-start(bf16[128,4,640]{0,2,1:T(8,128)(2,1)} %bitcast.227), calls=%async_computation.3 | async-start | bytes 1310720 | tf_op jit(solution)/shard_map/all_to_all | solution.py:70
  135.0 12.5 %copy-start.1 = (f32[3,5,4,128,128]{4,2,3,1,0:T(4,128)}, f32[3,5,4,128,128]{4,2,3,1,0:T(4,128)S(1)}, u32[]{:S(2)}) copy-start(f32[3,5,4,128,128]{4,2,3,1,0:T(4,128)S(1)} %bitcast_add_fusion.5) | copy-start | bytes 11796484 | tf_op jit(solution)/shard_map/while
  138.6 10.7 %copy-start.11 = (bf16[5,4,128,128]{3,2,1,0:T(8,128)(2,1)S(1)}, bf16[5,4,128,128]{3,2,1,0:T(8,128)(2,1)}, u32[]{:S(2)}) copy-start(bf16[5,4,128,128]{3,2,1,0:T(8,128)(2,1)} %copy-done.10) | copy-start | bytes 1966084 | tf_op jit(solution)/shard_map/while
  138.6 10.7 %copy-start.13 = (bf16[5,4,128,128]{3,2,1,0:T(8,128)(2,1)S(1)}, bf16[5,4,128,128]{3,2,1,0:T(8,128)(2,1)}, u32[]{:S(2)}) copy-start(bf16[5,4,128,128]{3,2,1,0:T(8,128)(2,1)} %copy-done.12) | copy-start | bytes 1966084 | tf_op jit(solution)/shard_map/while
  138.6 10.7 %copy-start.15 = (bf16[5,4,128,128]{2,3,0,1:T(8,128)(2,1)S(1)}, bf16[5,4,128,128]{2,3,0,1:T(8,128)(2,1)}, u32[]{:S(2)}) copy-start(bf16[5,4,128,128]{2,3,0,1:T(8,128)(2,1)} %copy-done.14) | copy-start | bytes 1966084 | tf_op jit(solution)/shard_map/while
  187.7 12.5 %copy-start.1 = (f32[3,5,4,128,128]{4,2,3,1,0:T(4,128)}, f32[3,5,4,128,128]{4,2,3,1,0:T(4,128)S(1)}, u32[]{:S(2)}) copy-start(f32[3,5,4,128,128]{4,2,3,1,0:T(4,128)S(1)} %bitcast_add_fusion.5) | copy-start | bytes 11796484 | tf_op jit(solution)/shard_map/while
  191.3 10.7 %copy-start.11 = (bf16[5,4,128,128]{3,2,1,0:T(8,128)(2,1)S(1)}, bf16[5,4,128,128]{3,2,1,0:T(8,128)(2,1)}, u32[]{:S(2)}) copy-start(bf16[5,4,128,128]{3,2,1,0:T(8,128)(2,1)} %copy-done.10) | copy-start | bytes 1966084 | tf_op jit(solution)/shard_map/while
  191.3 10.7 %copy-start.13 = (bf16[5,4,128,128]{3,2,1,0:T(8,128)(2,1)S(1)}, bf16[5,4,128,128]{3,2,1,0:T(8,128)(2,1)}, u32[]{:S(2)}) copy-start(bf16[5,4,128,128]{3,2,1,0:T(8,128)(2,1)} %copy-done.12) | copy-start | bytes 1966084 | tf_op jit(solution)/shard_map/while
  191.3 10.7 %copy-start.15 = (bf16[5,4,128,128]{2,3,0,1:T(8,128)(2,1)S(1)}, bf16[5,4,128,128]{2,3,0,1:T(8,128)(2,1)}, u32[]{:S(2)}) copy-start(bf16[5,4,128,128]{2,3,0,1:T(8,128)(2,1)} %copy-done.14) | copy-start | bytes 1966084 | tf_op jit(solution)/shard_map/while
  240.3 12.5 %copy-start.1 = (f32[3,5,4,128,128]{4,2,3,1,0:T(4,128)}, f32[3,5,4,128,128]{4,2,3,1,0:T(4,128)S(1)}, u32[]{:S(2)}) copy-start(f32[3,5,4,128,128]{4,2,3,1,0:T(4,128)S(1)} %bitcast_add_fusion.5) | copy-start | bytes 11796484 | tf_op jit(solution)/shard_map/while
  244.0 10.7 %copy-start.11 = (bf16[5,4,128,128]{3,2,1,0:T(8,128)(2,1)S(1)}, bf16[5,4,128,128]{3,2,1,0:T(8,128)(2,1)}, u32[]{:S(2)}) copy-start(bf16[5,4,128,128]{3,2,1,0:T(8,128)(2,1)} %copy-done.10) | copy-start | bytes 1966084 | tf_op jit(solution)/shard_map/while
  244.0 10.7 %copy-start.13 = (bf16[5,4,128,128]{3,2,1,0:T(8,128)(2,1)S(1)}, bf16[5,4,128,128]{3,2,1,0:T(8,128)(2,1)}, u32[]{:S(2)}) copy-start(bf16[5,4,128,128]{3,2,1,0:T(8,128)(2,1)} %copy-done.12) | copy-start | bytes 1966084 | tf_op jit(solution)/shard_map/while
  244.0 10.7 %copy-start.15 = (bf16[5,4,128,128]{2,3,0,1:T(8,128)(2,1)S(1)}, bf16[5,4,128,128]{2,3,0,1:T(8,128)(2,1)}, u32[]{:S(2)}) copy-start(bf16[5,4,128,128]{2,3,0,1:T(8,128)(2,1)} %copy-done.14) | copy-start | bytes 1966084 | tf_op jit(solution)/shard_map/while
  293.0 12.5 %copy-start.1 = (f32[3,5,4,128,128]{4,2,3,1,0:T(4,128)}, f32[3,5,4,128,128]{4,2,3,1,0:T(4,128)S(1)}, u32[]{:S(2)}) copy-start(f32[3,5,4,128,128]{4,2,3,1,0:T(4,128)S(1)} %bitcast_add_fusion.5) | copy-start | bytes 11796484 | tf_op jit(solution)/shard_map/while
  296.6 10.7 %copy-start.11 = (bf16[5,4,128,128]{3,2,1,0:T(8,128)(2,1)S(1)}, bf16[5,4,128,128]{3,2,1,0:T(8,128)(2,1)}, u32[]{:S(2)}) copy-start(bf16[5,4,128,128]{3,2,1,0:T(8,128)(2,1)} %copy-done.10) | copy-start | bytes 1966084 | tf_op jit(solution)/shard_map/while
  296.6 10.7 %copy-start.13 = (bf16[5,4,128,128]{3,2,1,0:T(8,128)(2,1)S(1)}, bf16[5,4,128,128]{3,2,1,0:T(8,128)(2,1)}, u32[]{:S(2)}) copy-start(bf16[5,4,128,128]{3,2,1,0:T(8,128)(2,1)} %copy-done.12) | copy-start | bytes 1966084 | tf_op jit(solution)/shard_map/while
  296.6 10.7 %copy-start.15 = (bf16[5,4,128,128]{2,3,0,1:T(8,128)(2,1)S(1)}, bf16[5,4,128,128]{2,3,0,1:T(8,128)(2,1)}, u32[]{:S(2)}) copy-start(bf16[5,4,128,128]{2,3,0,1:T(8,128)(2,1)} %copy-done.14) | copy-start | bytes 1966084 | tf_op jit(solution)/shard_map/while
  319.9 34.6 %copy-start.8 = (f32[3,5,4,128,128]{3,4,1,2,0:T(8,128)S(1)}, f32[3,5,4,128,128]{3,4,1,2,0:T(8,128)}, u32[]{:S(2)}) copy-start(f32[3,5,4,128,128]{3,4,1,2,0:T(8,128)} %copy.106) | copy-start | bytes 11796484
  319.9 34.6 %copy-start.9 = (f32[3,5,4,128,128]{3,4,1,2,0:T(8,128)S(1)}, f32[3,5,4,128,128]{3,4,1,2,0:T(8,128)}, u32[]{:S(2)}) copy-start(f32[3,5,4,128,128]{3,4,1,2,0:T(8,128)} %copy.107) | copy-start | bytes 11796484
  322.0 42.0 %copy-start.19 = (bf16[4,5,128,128]{2,3,1,0:T(8,128)(2,1)S(1)}, bf16[4,5,128,128]{2,3,1,0:T(8,128)(2,1)}, u32[]{:S(2)}) copy-start(bf16[4,5,128,128]{2,3,1,0:T(8,128)(2,1)} %get-tuple-element.90) | copy-start | bytes 1966084
  322.0 32.5 %collective-permute-start.2 = (bf16[2,5,4,128,128]{3,4,1,2,0:T(8,128)(2,1)S(1)}, bf16[2,5,4,128,128]{3,4,1,2,0:T(8,128)(2,1)S(1)}, u32[]{:S(2)}, u32[]{:S(2)}) collective-permute-start(bf16[2,5,4,128,128]{3,4,1,2,0:T(8,128)(2,1)S(1)} %fusion.54), channel_id=1, source_target_pairs={{4,0},{8,4},{12,8},{16,12},{20,16},{24,20},{28,24},{32,28},{36,32}... | collective-permute-start | bytes 3932168 | tf_op jit(solution)/shard_map/ppermute | solution.py:21
  356.0 49.7 %collective-permute-start.3 = (bf16[2,5,4,128,128]{3,4,1,2,0:T(8,128)(2,1)}, bf16[2,5,4,128,128]{3,4,1,2,0:T(8,128)(2,1)S(1)}, u32[]{:S(2)}, u32[]{:S(2)}) collective-permute-start(bf16[2,5,4,128,128]{3,4,1,2,0:T(8,128)(2,1)} %fusion.48), channel_id=1, source_target_pairs={{4,0},{8,4},{12,8},{16,12},{20,16},{24,20},{28,24},{32,28},{36,32}... | collective-permute-start | bytes 3932168 | tf_op jit(solution)/shard_map/ppermute | solution.py:21
  360.5 41.8 %all-to-all-start.5 = ((bf16[4,128,640]{1,2,0:T(8,128)(2,1)}), bf16[4,128,640]{1,2,0:T(8,128)(2,1)S(1)}, u32[]{:S(2)}, u32[]{:S(2)}) async-start(bf16[4,128,640]{1,2,0:T(8,128)(2,1)} %bitcast.33), calls=%async_computation.5 | async-start | bytes 1310720 | tf_op jit(solution)/shard_map/all_to_all | solution.py:111
  402.2 13.7 %all-to-all-start.4 = ((bf16[4,128,640]{2,1,0:T(8,128)(2,1)}), bf16[4,128,640]{2,1,0:T(8,128)(2,1)S(1)}, u32[]{:S(2)}, u32[]{:S(2)}) async-start(bf16[4,128,640]{2,1,0:T(8,128)(2,1)} %copy.103), calls=%async_computation.4 | async-start | bytes 1310720 | tf_op jit(solution)/shard_map/all_to_all | solution.py:110
  428.5 13.7 %all-to-all-start.7 = ((bf16[4,128,640]{1,2,0:T(8,128)(2,1)}), bf16[4,128,640]{1,2,0:T(8,128)(2,1)S(1)}, u32[]{:S(2)}, u32[]{:S(2)}) async-start(bf16[4,128,640]{1,2,0:T(8,128)(2,1)} %bitcast.48), calls=%async_computation.7 | async-start | bytes 1310720 | tf_op jit(solution)/shard_map/all_to_all | solution.py:113
  (42 other events, 178.3 us)
where the time goes:
time: 446 us; the launch traced here: 443 us
  waiting for transfers between devices  129 us (29%)
  matrix products  116 us (26%)
  local copies, waits for them, and re-layouts  107 us (24%)
  starting transfers between devices  33.2 us (7%)
  blocking collectives  25.2 us (6%)
  other arithmetic  23.6 us (5%)
  loops' own time  8.54 us (2%)
    ppermute x4, waiting for transfers between devices, shifted(): return lax.ppermute(block, axis, route)  61.6 us
    all_to_all x1, waiting for transfers between devices, shards(): lax.all_to_all(dq_loc, 'head', split_axis=0, concat_axis=1, tiled=True)  37.2 us
    dot_general x4, matrix products, tile_pass(): jnp.einsum('hwstd,wsk->whktd', dkeys, onehot, precision=highest)  35.4 us
    dot_general x4, matrix products, tile_pass(): jnp.einsum('hwstd,wsk->whktd', dvals, onehot, precision=highest)  35.3 us
    while x112, local copies, waits for them, and re-layouts  22.4 us
    gather x12, local copies, waits for them, and re-layouts, tile_pass(): jnp.take(keys_all[lag], chosen[lag], axis=1)  16.4 us
    gather x12, local copies, waits for them, and re-layouts, tile_pass(): jnp.take(vals_all[lag], chosen[lag], axis=1)  16.4 us
    unnamed x31, local copies, waits for them, and re-layouts  16.2 us
  transfers between devices with their start and end apart: 10, of which 8 were waited for; matrix products, arithmetic and copies ran while one was open for 5% of the time, Pallas kernels for 0%

commit v1 on v0

v1 whole, which is shorter than its diff:
```python
import functools
import math

import jax
import jax.numpy as jnp
from jax import lax
from jax.experimental import pallas as pl
from jax.experimental.pallas import tpu as pltpu
from jax.sharding import PartitionSpec as P

HD = 128
TILE = 128
QT = 4
SEL = 3
W = 3
QH = 2
QB = QT // QH * TILE
NEG = -1e30
SCALE = 1.0 / math.sqrt(HD)
LOG2E = 1.0 / math.log(2.0)
MESH = pl.DeviceIdType.MESH
BF = jnp.bfloat16
F32 = jnp.float32


def kernel(
    n, heads,
    pat_ref, win_ref, q_ref, k_ref, v_ref, g_ref,
    o_ref, dq_ref, dk_ref, dv_ref,
    qg, kv, bias, kt, vt, score, pt, dst, keep0, keep1,
    a_out, a_in, b_out, b_in, outb,
    in_send, kv_in, qg_in, own_send, lag1_in, fwd_send, lag2_in,
    a_send, a_recv, b_send, b_recv, out_send, out_recv,
):
    f = lax.axis_index("tm")
    j = lax.axis_index("head")
    half = n // 2

    def group_of(seat):
        return lax.rem(seat + 2 * (f // half), QT)

    nxt = (f + 1, lax.rem(j + 2 * ((f + 1) // half - f // half), QT))
    prv = (f - 1, lax.rem(j + 2 * (f // half - (f + half - 1) // half + 1), QT))

    barrier = pltpu.get_barrier_semaphore()
    for d in range(1, QT):
        pl.semaphore_signal(barrier, inc=1, device_id=(f, lax.rem(j + d, QT)), device_id_type=MESH)

    @pl.when(f < n - 1)
    def _():
        pl.semaphore_signal(barrier, inc=1, device_id=nxt, device_id_type=MESH)

    @pl.when(f > 0)
    def _():
        pl.semaphore_signal(barrier, inc=1, device_id=prv, device_id_type=MESH)

    pl.semaphore_wait(barrier, QT - 1 + (f + n - 1) // n + (2 * n - 2 - f) // n)

    def columns(group, i):
        return pl.ds(pl.multiple_of((group * heads + i) * HD, HD), HD)

    def wait_for(ref, sem):
        pltpu.make_async_copy(ref, ref, sem).wait()

    def send(src, dst, ssem, rsem, device):
        pltpu.make_async_remote_copy(
            src_ref=src, dst_ref=dst, send_sem=ssem, recv_sem=rsem,
            device_id=device, device_id_type=MESH,
        ).start()

    def enter(i, refs, slot, sem):
        for d in range(1, QT):
            seat = lax.rem(j + d, QT)
            for a, ref in enumerate(refs):
                send(ref.at[:, columns(group_of(seat), i)], slot.at[a, j],
                     in_send.at[i], sem, (f, seat))
        for a, ref in enumerate(refs):
            pltpu.make_async_copy(ref.at[:, columns(group_of(j), i)], slot.at[a, j], sem).start()

    @pl.loop(0, heads)
    def _(i):
        enter(i, (k_ref, v_ref), kv.at[i, 0], kv_in.at[i])

        @pl.when(f < n - 1)
        def _():
            for a, ref in enumerate((k_ref, v_ref)):
                send(ref.at[:, columns(group_of(j), i)], kv.at[i, 1, a, j],
                     own_send.at[i], lag1_in.at[i], nxt)

        enter(i, (q_ref, g_ref), qg.at[i], qg_in.at[i])

    lane = lax.broadcasted_iota(jnp.int32, (1, QB), 1)
    limit = win_ref[f]
    for h in range(QH):
        for lag in range(W):
            for t in range(QT):
                pair = []
                for tile in (2 * h, 2 * h + 1):
                    hit = pat_ref[lag, tile, 0] == t
                    for s in range(1, SEL):
                        hit = hit | (pat_ref[lag, tile, s] == t)
                    hit = hit & (lag <= f) & (lag < limit)
                    pair.append(jnp.where(hit, 0.0, NEG).astype(F32))
                bias[h, lag * QT + t] = jnp.where(lane < TILE, pair[0], pair[1])

    @pl.when(f == 0)
    def _():
        @pl.loop(0, heads)
        def _(i):
            kv[i, 1] = jnp.zeros(kv.shape[2:], BF)
            kv[i, 2] = jnp.zeros(kv.shape[2:], BF)

    @pl.when(f == n - 1)
    def _():
        @pl.loop(0, heads)
        def _(i):
            a_in[i] = jnp.zeros(a_in.shape[1:], BF)
            b_in[i] = jnp.zeros(b_in.shape[1:], BF)

    def own(i):
        wait_for(kv.at[i, 0], kv_in.at[i])

        @pl.when(f < n - 1)
        def _():
            for d in range(1, QT):
                t = lax.rem(j + d, QT)
                for a in range(2):
                    send(kv.at[i, 0, a, t], kv.at[i, 1, a, t], own_send.at[i], lag1_in.at[i], nxt)

    def forward(i):
        @pl.when(f > 0)
        def _():
            wait_for(kv.at[i, 1], lag1_in.at[i])

        @pl.when(f < n - 1)
        def _():
            send(kv.at[i, 1], kv.at[i, 2], fwd_send.at[i], lag2_in.at[i], nxt)

    def leave(i, a):
        outs = (o_ref, dq_ref, dk_ref, dv_ref)
        where_to = outs[a].at[:, columns(group_of(j), i)]
        for d in range(1, QT):
            seat = lax.rem(j + d, QT)
            send(outb.at[i, a, seat], where_to, out_send.at[i], out_recv.at[a], (f, seat))
        pltpu.make_async_copy(outb.at[i, a, j], where_to, out_recv.at[a]).start()

    def flat(ref):
        return ref[...].reshape(QT * TILE, HD)

    def attend(i):
        for lag in range(W):
            kt[lag] = flat(kv.at[i, lag, 0]).T
            vt[lag] = flat(kv.at[i, lag, 1]).T

        @pl.loop(0, QH)
        def _(h):
            two = pl.ds(2 * h, 2)
            qh = qg[i, 0, two].reshape(QB, HD)
            gh = qg[i, 1, two].reshape(QB, HD)
            top = None
            for lag in range(W):
                for t in range(QT):
                    r = lag * QT + t
                    s = lax.dot_general(kv[i, lag, 0, t], qh, (((1,), (1,)), ((), ())),
                                        preferred_element_type=F32)
                    score[r] = s
                    here = jnp.max(s, axis=0, keepdims=True) + bias[h, r]
                    top = here if top is None else jnp.maximum(top, here)
            factor = SCALE * LOG2E
            total = jnp.zeros((1, QB), F32)
            for r in range(W * QT):
                e = jnp.exp2(score[r] * factor + (bias[h, r] - top) * factor)
                score[r] = e
                total = total + jnp.sum(e, axis=0, keepdims=True)
            inverse = 1.0 / total
            for r in range(W * QT):
                pt[h, r] = (score[r] * inverse).astype(BF)
            out = jnp.zeros((HD, QB), F32)
            for lag in range(W):
                probs = pt[h, lag * QT:(lag + 1) * QT].reshape(QT * TILE, QB)
                out = out + jnp.dot(vt[lag], probs, preferred_element_type=F32)
            delta = jnp.sum(gh.T.astype(F32) * out, axis=0, keepdims=True)
            outb[i, 0, two] = out.astype(BF).T.reshape(2, TILE, HD)
            scaled = inverse * SCALE
            for lag in range(W):
                for t in range(QT):
                    r = lag * QT + t
                    dp = lax.dot_general(kv[i, lag, 1, t], gh, (((1,), (1,)), ((), ())),
                                         preferred_element_type=F32)
                    dst[h, r] = (score[r] * scaled * (dp - delta)).astype(BF)
            dq = jnp.zeros((HD, QB), F32)
            for lag in range(W):
                ds = dst[h, lag * QT:(lag + 1) * QT].reshape(QT * TILE, QB)
                dq = dq + jnp.dot(kt[lag], ds, preferred_element_type=F32)
            outb[i, 1, two] = dq.astype(BF).T.reshape(2, TILE, HD)

        for lag in range(W):
            for a, (grads, rows) in enumerate(((dst, qg.at[i, 0]), (pt, qg.at[i, 1]))):
                acc = jnp.zeros((QT * TILE, HD), F32)
                for h in range(QH):
                    block = grads[h, lag * QT:(lag + 1) * QT].reshape(QT * TILE, QB)
                    acc = acc + jnp.dot(block, rows[2 * h:2 * h + 2].reshape(QB, HD),
                                        preferred_element_type=F32)
                acc = acc.reshape(QT, TILE, HD)
                if lag == 0:
                    keep0[i, a] = acc
                elif lag == 1:
                    keep1[i, a] = acc
                else:
                    a_out[i, a] = acc.astype(BF)

    def compute(i):
        wait_for(qg.at[i], qg_in.at[i])

        @pl.when(f > 0)
        def _():
            wait_for(kv.at[i, 2], lag2_in.at[i])

        attend(i)

        @pl.when(f > 0)
        def _():
            for a in range(2):
                send(a_out.at[i, a], a_in.at[i, a], a_send.at[i, a], a_recv.at[i, a], prv)

        leave(i, 0)
        leave(i, 1)

    def chain(i):
        for a in range(2):
            @pl.when(f < n - 1)
            def _():
                wait_for(a_in.at[i, a], a_recv.at[i, a])

            b_out[i, a] = (keep1[i, a] + a_in[i, a].astype(F32)).astype(BF)

            @pl.when(f > 0)
            def _():
                send(b_out.at[i, a], b_in.at[i, a], b_send.at[i, a], b_recv.at[i, a], prv)

    def finish(i):
        for a in range(2):
            @pl.when(f < n - 1)
            def _():
                wait_for(b_in.at[i, a], b_recv.at[i, a])

            outb[i, 2 + a] = (keep0[i, a] + b_in[i, a].astype(F32)).astype(BF)
            leave(i, 2 + a)

    own(0)

    @pl.loop(0, heads + 3)
    def _(s):
        @pl.when(s + 1 < heads)
        def _():
            own(s + 1)

        @pl.when(s < heads)
        def _():
            forward(s)

        @pl.when((s >= 1) & (s < heads + 1))
        def _():
            compute(s - 1)

        @pl.when((s >= 2) & (s < heads + 2))
        def _():
            chain(s - 2)

        @pl.when(s >= 3)
        def _():
            finish(s - 3)

    @pl.loop(0, heads)
    def _(i):
        wait_for(outb.at[i, 0:3], in_send.at[i])
        wait_for(outb.at[i, 0:3], out_send.at[i])

        @pl.when(f < n - 1)
        def _():
            wait_for(kv.at[i, 0], own_send.at[i])
            wait_for(kv.at[i, 1], fwd_send.at[i])

        @pl.when(f > 0)
        def _():
            for a in range(2):
                wait_for(a_out.at[i, a], a_send.at[i, a])
                wait_for(b_out.at[i, a], b_send.at[i, a])

    for a, ref in enumerate((o_ref, dq_ref, dk_ref, dv_ref)):
        wait_for(ref, out_recv.at[a])


def shards(n, query, keys, values, grad_out, tile_pattern, window):
    rows, width = query.shape
    heads = width // HD // QT
    blocks = (QT, TILE, HD)
    dma = pltpu.SemaphoreType.DMA
    scratch = [
        pltpu.VMEM((heads, 2) + blocks, BF),
        pltpu.VMEM((heads, W, 2) + blocks, BF),
        pltpu.VMEM((QH, W * QT, 1, QB), F32),
        pltpu.VMEM((W, HD, QT * TILE), BF),
        pltpu.VMEM((W, HD, QT * TILE), BF),
        pltpu.VMEM((W * QT, TILE, QB), F32),
        pltpu.VMEM((QH, W * QT, TILE, QB), BF),
        pltpu.VMEM((QH, W * QT, TILE, QB), BF),
        pltpu.VMEM((heads, 2) + blocks, F32),
        pltpu.VMEM((heads, 2) + blocks, F32),
        pltpu.VMEM((heads, 2) + blocks, BF),
        pltpu.VMEM((heads, 2) + blocks, BF),
        pltpu.VMEM((heads, 2) + blocks, BF),
        pltpu.VMEM((heads, 2) + blocks, BF),
        pltpu.VMEM((heads, 4) + blocks, BF),
        dma((heads,)), dma((heads,)), dma((heads,)),
        dma((heads,)), dma((heads,)), dma((heads,)), dma((heads,)),
        dma((heads, 2)), dma((heads, 2)), dma((heads, 2)), dma((heads, 2)),
        dma((heads,)), dma((4,)),
    ]
    smem = pl.BlockSpec(memory_space=pltpu.SMEM)
    anywhere = pl.BlockSpec(memory_space=pl.ANY)
    return pl.pallas_call(
        functools.partial(kernel, n, heads),
        out_shape=[jax.ShapeDtypeStruct((rows, width), BF)] * 4,
        in_specs=[smem, smem] + [anywhere] * 4,
        out_specs=[anywhere] * 4,
        scratch_shapes=scratch,
        compiler_params=pltpu.CompilerParams(
            collective_id=0, has_side_effects=True, vmem_limit_bytes=56 * 1024 * 1024
        ),
    )(tile_pattern, window, query, keys, values, grad_out)


def solution(mesh):
    rows = P(("tm", "head"), None)
    return jax.shard_map(
        functools.partial(shards, mesh.shape["tm"]),
        mesh=mesh,
        in_specs=(rows, rows, rows, rows, P(), P()),
        out_specs=(rows, rows, rows, rows),
        check_vma=False,
    )
```

time: 446 us -> 109 us (0.24)
  the two profiles are of different devices: /device:TPU:246 before, /device:TPU:17 now
where the time goes in v1:
time: 109 us
  Pallas kernels  103 us (94%)
  local copies, waits for them, and re-layouts  5.52 us (5%)
    pallas_call x1, Pallas kernels, shards(): pl.pallas_call(functools.partial(kernel, n, heads), out_shape=[jax.ShapeD...  103 us
    unnamed x10, local copies, waits for them, and re-layouts  5.52 us

profile of v1, /device:TPU:17, one launch (start us, length us, event | category | flops | bytes accessed | tf_op | source)
XLA Modules:
  0.0 109.2 jit_solution(14710958221902551037)
XLA Ops:
  0.6 103.1 %shard_map.93 = (bf16[128,2560]{1,0:T(8,128)(2,1)}, bf16[128,2560]{1,0:T(8,128)(2,1)}, bf16[128,2560]{1,0:T(8,128)(2,1)}, bf16[128,2560]{1,0:T(8,128)(2,1)}) custom-call(s32[3,4,3]{2,1,0:T(4,128)} %pat_ref.1, s32[64]{0:T(128)} %win_ref.1, bf16[128,2560]{1,0:T(8,128)(2,1)} %q_ref.1, bf16[128,2560]{1,0:T(8,128)(2,1)} %k_ref.1, bf16[128,2560]{1,0:T(8,128)(2,1)} %v_ref.1, ...), custom_call_target="tpu_custom_call" | custom-call | tf_op jit(solution)/shard_map/pallas_call | solution.py:322
  103.7 0.0 copy-start.2
  103.7 2.0 %copy.14 = bf16[128,2560]{1,0:T(8,128)(2,1)} copy(bf16[128,2560]{1,0:T(8,128)(2,1)} %get-tuple-element.8) | data formatting | bytes 1310720
  105.8 0.0 copy-done.2
  105.8 0.0 copy-start.1
  105.8 0.8 copy.15
  106.6 0.5 copy-done.1
  107.1 0.0 copy-start
  107.1 0.8 copy.16
  107.9 0.5 copy-done
  108.4 0.8 copy.17
Async XLA Ops:
  103.7 2.0 %copy-start.2 = (bf16[128,2560]{1,0:T(8,128)(2,1)S(1)}, bf16[128,2560]{1,0:T(8,128)(2,1)}, u32[]{:S(2)}) copy-start(bf16[128,2560]{1,0:T(8,128)(2,1)} %get-tuple-element.9) | copy-start | bytes 1966084
  105.8 1.3 %copy-start.1 = (bf16[128,2560]{1,0:T(8,128)(2,1)S(1)}, bf16[128,2560]{1,0:T(8,128)(2,1)}, u32[]{:S(2)}) copy-start(bf16[128,2560]{1,0:T(8,128)(2,1)} %get-tuple-element.10) | copy-start | bytes 1966084
  107.1 1.3 %copy-start = (bf16[128,2560]{1,0:T(8,128)(2,1)S(1)}, bf16[128,2560]{1,0:T(8,128)(2,1)}, u32[]{:S(2)}) copy-start(bf16[128,2560]{1,0:T(8,128)(2,1)} %get-tuple-element.11) | copy-start | bytes 1966084

commit v2 on v0

v2 whole, which is shorter than its diff:
```python
import functools
import math

import jax
import jax.numpy as jnp
from jax import lax
from jax.experimental import pallas as pl
from jax.experimental.pallas import tpu as pltpu
from jax.sharding import PartitionSpec as P

HD = 128
TILE = 128
QT = 4
SEL = 3
W = 3
QH = 2
QB = QT // QH * TILE
NEG = -1e30
SCALE = 1.0 / math.sqrt(HD)
FACTOR = SCALE / math.log(2.0)
MESH = pl.DeviceIdType.MESH
BF = jnp.bfloat16
F32 = jnp.float32


def kernel(
    n, chip_heads,
    pat_ref, win_ref, q_ref, k_ref, v_ref, g_ref,
    o_ref, dq_ref, dk_ref, dv_ref,
    qg, kv, bias, kt, vt, score, pt, dst, gs, acc, g_out, g_in, outb,
    in_send, kv_in, qg_in, next_send, next_in, g_send, g_recv, out_send, out_recv,
):
    f = lax.axis_index("tm")
    seat = lax.axis_index("head")
    half = n // 2
    pair, side = f // 2, lax.rem(f, 2)
    pairs = n // 2
    most = (chip_heads + 1) // 2

    def count(at):
        return (chip_heads + 1 - lax.rem(at, 2)) // 2

    def first_head(other, at):
        row = lax.rem(other + pair, 2)
        column = lax.rem(at // 2 + f // half, 2)
        return (row * 2 + column) * chip_heads + lax.rem(at, 2) * most

    def linked(step):
        frame = 2 * (pair + step) + 1 - side
        turn = (frame + n) // half - (f + n) // half
        return (frame, lax.rem(seat + 2 * turn + 2 * QT, QT))

    nxt, prv = linked(1), linked(-1)
    has_next = pair < pairs - 1
    has_prev = pair > 0
    mine = count(seat)
    peers = [(dx, dj) for dj in range(QT) for dx in (1, 0)]

    def peer(dx, dj):
        return lax.rem(side + dx, 2), lax.rem(seat + dj, QT)

    barrier = pltpu.get_barrier_semaphore()
    for dx, dj in peers:
        if dx or dj:
            other, at = peer(dx, dj)
            pl.semaphore_signal(barrier, inc=1, device_id=(2 * pair + other, at), device_id_type=MESH)

    @pl.when(has_next)
    def _():
        pl.semaphore_signal(barrier, inc=1, device_id=nxt, device_id_type=MESH)

    @pl.when(has_prev)
    def _():
        pl.semaphore_signal(barrier, inc=1, device_id=prv, device_id_type=MESH)

    pl.semaphore_wait(barrier, 2 * QT - 1 + (pair + pairs - 1) // pairs + (2 * pairs - 2 - pair) // pairs)

    def columns(head):
        return pl.ds(pl.multiple_of(head * HD, HD), HD)

    def wait_for(ref, sem):
        pltpu.make_async_copy(ref, ref, sem).wait()

    def send(src, dst, ssem, rsem, device):
        pltpu.make_async_remote_copy(
            src_ref=src, dst_ref=dst, send_sem=ssem, recv_sem=rsem,
            device_id=device, device_id_type=MESH,
        ).start()

    def enter(i, refs, slot, sem):
        for dx, dj in peers:
            other, at = peer(dx, dj)
            cols = columns(first_head(other, at) + i)

            @pl.when(i < count(at))
            def _():
                for a, ref in enumerate(refs):
                    if dx or dj:
                        send(ref.at[:, cols], slot.at[a, seat], in_send.at[i, 2 * dj + dx], sem,
                             (2 * pair + other, at))
                    else:
                        pltpu.make_async_copy(ref.at[:, cols], slot.at[a, seat], sem).start()

    @pl.loop(0, most)
    def _(i):
        enter(i, (k_ref, v_ref), kv.at[i, 1 - side], kv_in.at[i])
        enter(i, (q_ref, g_ref), qg.at[i, side], qg_in.at[i])

    lane = lax.broadcasted_iota(jnp.int32, (1, QB), 1)
    for x in range(2):
        frame = 2 * pair + x
        limit = win_ref[frame]
        for h in range(QH):
            for lag in range(W):
                for t in range(QT):
                    both = []
                    for tile in (2 * h, 2 * h + 1):
                        hit = pat_ref[lag, tile, 0] == t
                        for s in range(1, SEL):
                            hit = hit | (pat_ref[lag, tile, s] == t)
                        hit = hit & (lag <= frame) & (lag < limit)
                        both.append(jnp.where(hit, 0.0, NEG).astype(F32))
                    bias[x, h, lag * QT + t] = jnp.where(lane < TILE, both[0], both[1])

    @pl.loop(0, most)
    def _(i):
        acc[i] = jnp.zeros(acc.shape[1:], F32)

        @pl.when(pair == 0)
        def _():
            kv[i, 2] = jnp.zeros(kv.shape[2:], BF)
            kv[i, 3] = jnp.zeros(kv.shape[2:], BF)

        @pl.when(pair == pairs - 1)
        def _():
            g_in[i] = jnp.zeros(g_in.shape[1:], BF)

    def own(i):
        wait_for(kv.at[i, 0:2], kv_in.at[i])

        @pl.when(has_next)
        def _():
            for s in range(2):
                send(kv.at[i, s], kv.at[i, 2 + s], next_send.at[i, s], next_in.at[i, s], nxt)

    def leave(i, x, a):
        ref = (o_ref, dq_ref, dk_ref, dv_ref)[a]
        where_to = ref.at[:, columns(first_head(side, seat) + i)]
        for dj in range(QT):
            at = lax.rem(seat + dj, QT)
            if dj:
                send(outb.at[i, x, a, at], where_to, out_send.at[i, x, a, dj], out_recv.at[a],
                     (2 * pair + x, at))
            else:
                @pl.when(x == side)
                def _():
                    pltpu.make_async_copy(outb.at[i, x, a, at], where_to, out_recv.at[a]).start()

                @pl.when(x != side)
                def _():
                    send(outb.at[i, x, a, at], where_to, out_send.at[i, x, a, dj], out_recv.at[a],
                         (2 * pair + 1 - side, at))

    def nt(a, b):
        return lax.dot_general(a, b, (((1,), (1,)), ((), ())), preferred_element_type=F32)

    def mm(a, b):
        return jnp.dot(a, b, preferred_element_type=F32)

    def fold(block, op):
        return op(block.reshape(TILE // 8, 8, QB), axis=0)

    def attend(i, x):
        base = 1 - x

        def turn(slot):
            kt[slot] = kv[i, slot, 0].reshape(QT * TILE, HD).T
            vt[slot] = kv[i, slot, 1].reshape(QT * TILE, HD).T

        @pl.when(x == 1)
        def _():
            for slot in range(3):
                turn(slot)

        @pl.when(x == 0)
        def _():
            turn(3)

        for h in range(QH):
            lanes = slice(h * QB, (h + 1) * QB)
            qh = qg[i, x, 0, 2 * h:2 * h + 2].reshape(QB, HD)
            gh = qg[i, x, 1, 2 * h:2 * h + 2].reshape(QB, HD)
            top = None
            for lag in range(W):
                for t in range(QT):
                    r = lag * QT + t
                    s = nt(kv[i, base + lag, 0, t], qh)
                    score[h, r] = s
                    here = fold(s, jnp.max) + bias[x, h, r]
                    top = here if top is None else jnp.maximum(top, here)
            top = jnp.max(top, axis=0, keepdims=True)
            total = None
            for r in range(W * QT):
                e = jnp.exp2(score[h, r] * FACTOR + (bias[x, h, r] - top) * FACTOR)
                pt[r, :, lanes] = e.astype(BF)
                here = fold(e, jnp.sum)
                total = here if total is None else total + here
            inverse = 1.0 / jnp.sum(total, axis=0, keepdims=True)
            out = None
            for lag in range(W):
                probs = pt[lag * QT:(lag + 1) * QT, :, lanes].reshape(QT * TILE, QB)
                here = mm(vt[base + lag], probs)
                out = here if out is None else out + here
            out = out * inverse
            scaled = (gh.T.astype(F32) * inverse).astype(BF)
            delta = jnp.sum(scaled.astype(F32) * out, axis=0, keepdims=True)
            outb[i, x, 0, 2 * h:2 * h + 2] = out.astype(BF).T.reshape(2, TILE, HD)
            back = scaled.T
            gs[lanes] = back
            for lag in range(W):
                for t in range(QT):
                    r = lag * QT + t
                    dp = nt(kv[i, base + lag, 1, t], back) - delta
                    dst[r, :, lanes] = dp.astype(BF) * pt[r, :, lanes]
            dq = None
            for lag in range(W):
                ds = dst[lag * QT:(lag + 1) * QT, :, lanes].reshape(QT * TILE, QB)
                here = mm(kt[base + lag], ds)
                dq = here if dq is None else dq + here
            outb[i, x, 1, 2 * h:2 * h + 2] = (dq * SCALE).astype(BF).T.reshape(2, TILE, HD)

        rows = qg[i, x, 0].reshape(QT * TILE, HD)
        for lag in range(W):
            block = dst[lag * QT:(lag + 1) * QT].reshape(QT * TILE, QT * TILE)
            acc[i, base + lag, 0] += (mm(block, rows) * SCALE).reshape(QT, TILE, HD)
            block = pt[lag * QT:(lag + 1) * QT].reshape(QT * TILE, QT * TILE)
            acc[i, base + lag, 1] += mm(block, gs[...]).reshape(QT, TILE, HD)

    def finish(i):
        for s in range(2):
            for a in range(2):
                @pl.when(has_next)
                def _():
                    wait_for(g_in.at[i, s, a], g_recv.at[i, s, a])

                outb[i, 1 - s, 2 + a] = (acc[i, s, a] + g_in[i, s, a].astype(F32)).astype(BF)
                leave(i, 1 - s, 2 + a)

    own(0)

    @pl.loop(0, 2 * most + 2)
    def _(u):
        i, odd = u // 2, lax.rem(u, 2)

        @pl.when(i < mine)
        def _():
            @pl.when(odd == 0)
            def _():
                wait_for(qg.at[i], qg_in.at[i])

            @pl.when(has_prev)
            def _():
                wait_for(kv.at[i, 2 + odd], next_in.at[i, odd])

            attend(i, 1 - odd)
            leave(i, 1 - odd, 0)
            leave(i, 1 - odd, 1)

            @pl.when((odd == 1) & has_prev)
            def _():
                for s in range(2):
                    for a in range(2):
                        g_out[i, s, a] = acc[i, 2 + s, a].astype(BF)
                        send(g_out.at[i, s, a], g_in.at[i, s, a], g_send.at[i, s, a],
                             g_recv.at[i, s, a], prv)

        @pl.when((odd == 0) & (i + 1 < mine))
        def _():
            own(i + 1)

        @pl.when((odd == 1) & (i >= 1) & (i < mine + 1))
        def _():
            finish(i - 1)

    @pl.loop(0, most)
    def _(i):
        for dx, dj in peers:
            if dx or dj:
                @pl.when(i < count(peer(dx, dj)[1]))
                def _():
                    wait_for(qg.at[i, 0, 0], in_send.at[i, 2 * dj + dx])

        @pl.when(i < mine)
        def _():
            for x in range(2):
                for a in range(4):
                    for dj in range(QT):
                        if dj:
                            wait_for(outb.at[i, x, a, dj], out_send.at[i, x, a, dj])
                        else:
                            @pl.when(x != side)
                            def _():
                                wait_for(outb.at[i, x, a, dj], out_send.at[i, x, a, dj])

            for s in range(2):
                @pl.when(has_next)
                def _():
                    wait_for(kv.at[i, s], next_send.at[i, s])

                @pl.when(has_prev)
                def _():
                    for a in range(2):
                        wait_for(g_out.at[i, s, a], g_send.at[i, s, a])

    for a, ref in enumerate((o_ref, dq_ref, dk_ref, dv_ref)):
        wait_for(ref, out_recv.at[a])


def shards(n, query, keys, values, grad_out, tile_pattern, window):
    rows, width = query.shape
    chip_heads = width // HD // 4
    most = (chip_heads + 1) // 2
    blocks = (QT, TILE, HD)
    dma = pltpu.SemaphoreType.DMA
    scratch = [
        pltpu.VMEM((most, 2, 2) + blocks, BF),
        pltpu.VMEM((most, 4, 2) + blocks, BF),
        pltpu.VMEM((2, QH, W * QT, 1, QB), F32),
        pltpu.VMEM((4, HD, QT * TILE), BF),
        pltpu.VMEM((4, HD, QT * TILE), BF),
        pltpu.VMEM((QH, W * QT, TILE, QB), F32),
        pltpu.VMEM((W * QT, TILE, QT * TILE), BF),
        pltpu.VMEM((W * QT, TILE, QT * TILE), BF),
        pltpu.VMEM((QT * TILE, HD), BF),
        pltpu.VMEM((most, 4, 2) + blocks, F32),
        pltpu.VMEM((most, 2, 2) + blocks, BF),
        pltpu.VMEM((most, 2, 2) + blocks, BF),
        pltpu.VMEM((most, 2, 4) + blocks, BF),
        dma((most, 8)), dma((most,)), dma((most,)),
        dma((most, 2)), dma((most, 2)),
        dma((most, 2, 2)), dma((most, 2, 2)),
        dma((most, 2, 4, QT)), dma((4,)),
    ]
    smem = pl.BlockSpec(memory_space=pltpu.SMEM)
    anywhere = pl.BlockSpec(memory_space=pl.ANY)
    return pl.pallas_call(
        functools.partial(kernel, n, chip_heads),
        out_shape=[jax.ShapeDtypeStruct((rows, width), BF)] * 4,
        in_specs=[smem, smem] + [anywhere] * 4,
        out_specs=[anywhere] * 4,
        scratch_shapes=scratch,
        compiler_params=pltpu.CompilerParams(
            collective_id=0, has_side_effects=True, vmem_limit_bytes=56 * 1024 * 1024
        ),
    )(tile_pattern, window, query, keys, values, grad_out)


def solution(mesh):
    rows = P(("tm", "head"), None)
    return jax.shard_map(
        functools.partial(shards, mesh.shape["tm"]),
        mesh=mesh,
        in_specs=(rows, rows, rows, rows, P(), P()),
        out_specs=(rows, rows, rows, rows),
        check_vma=False,
    )
```

time: 446 us -> 102 us (0.23)
  the two profiles are of different devices: /device:TPU:246 before, /device:TPU:17 now
where the time goes in v2:
time: 102 us; the launch traced here: 100 us
  Pallas kernels  94.1 us (92%)
  local copies, waits for them, and re-layouts  5.52 us (5%)
    pallas_call x1, Pallas kernels, shards(): pl.pallas_call(functools.partial(kernel, n, chip_heads), out_shape=[jax.S...  94.1 us
    unnamed x10, local copies, waits for them, and re-layouts  5.52 us

profile of v2, /device:TPU:17, one launch (start us, length us, event | category | flops | bytes accessed | tf_op | source)
XLA Modules:
  0.0 100.3 jit_solution(1819731457430763619)
XLA Ops:
  0.6 94.1 %shard_map.93 = (bf16[128,2560]{1,0:T(8,128)(2,1)}, bf16[128,2560]{1,0:T(8,128)(2,1)}, bf16[128,2560]{1,0:T(8,128)(2,1)}, bf16[128,2560]{1,0:T(8,128)(2,1)}) custom-call(s32[3,4,3]{2,1,0:T(4,128)} %pat_ref.1, s32[64]{0:T(128)} %win_ref.1, bf16[128,2560]{1,0:T(8,128)(2,1)} %q_ref.1, bf16[128,2560]{1,0:T(8,128)(2,1)} %k_ref.1, bf16[128,2560]{1,0:T(8,128)(2,1)} %v_ref.1, ...), custom_call_target="tpu_custom_call" | custom-call | tf_op jit(solution)/shard_map/pallas_call | solution.py:346
  94.8 0.0 copy-start.2
  94.8 2.0 %copy.14 = bf16[128,2560]{1,0:T(8,128)(2,1)} copy(bf16[128,2560]{1,0:T(8,128)(2,1)} %get-tuple-element.8) | data formatting | bytes 1310720
  96.8 0.0 copy-done.2
  96.8 0.0 copy-start.1
  96.8 0.8 copy.15
  97.7 0.5 copy-done.1
  98.1 0.0 copy-start
  98.1 0.8 copy.16
  99.0 0.5 copy-done
  99.5 0.8 copy.17
Async XLA Ops:
  94.8 2.0 %copy-start.2 = (bf16[128,2560]{1,0:T(8,128)(2,1)S(1)}, bf16[128,2560]{1,0:T(8,128)(2,1)}, u32[]{:S(2)}) copy-start(bf16[128,2560]{1,0:T(8,128)(2,1)} %get-tuple-element.9) | copy-start | bytes 1966084
  96.8 1.3 %copy-start.1 = (bf16[128,2560]{1,0:T(8,128)(2,1)S(1)}, bf16[128,2560]{1,0:T(8,128)(2,1)}, u32[]{:S(2)}) copy-start(bf16[128,2560]{1,0:T(8,128)(2,1)} %get-tuple-element.10) | copy-start | bytes 1966084
  98.1 1.3 %copy-start = (bf16[128,2560]{1,0:T(8,128)(2,1)S(1)}, bf16[128,2560]{1,0:T(8,128)(2,1)}, u32[]{:S(2)}) copy-start(bf16[128,2560]{1,0:T(8,128)(2,1)} %get-tuple-element.11) | copy-start | bytes 1966084

commit v3 on v2

--- a/solution.py
+++ b/solution.py
@@ -55,6 +55,7 @@
     has_prev = pair > 0
     mine = count(seat)
     peers = [(dx, dj) for dj in range(QT) for dx in (1, 0)]
+    arrivals = [(dx, QT - dj if dj else 0) for dx, dj in peers]
 
     def peer(dx, dj):
         return lax.rem(side + dx, 2), lax.rem(seat + dj, QT)
@@ -87,13 +88,14 @@
             device_id=device, device_id_type=MESH,
         ).start()
 
-    def enter(i, refs, slot, sem):
+    def enter(i, refs, slot, sem_of):
         for dx, dj in peers:
             other, at = peer(dx, dj)
             cols = columns(first_head(other, at) + i)
 
             @pl.when(i < count(at))
             def _():
+                sem = sem_of(dx, dj)
                 for a, ref in enumerate(refs):
                     if dx or dj:
                         send(ref.at[:, cols], slot.at[a, seat], in_send.at[i, 2 * dj + dx], sem,
@@ -101,10 +103,25 @@
                     else:
                         pltpu.make_async_copy(ref.at[:, cols], slot.at[a, seat], sem).start()
 
-    @pl.loop(0, most)
-    def _(i):
-        enter(i, (k_ref, v_ref), kv.at[i, 1 - side], kv_in.at[i])
-        enter(i, (q_ref, g_ref), qg.at[i, side], qg_in.at[i])
+    def enter_kv(i):
+        enter(i, (k_ref, v_ref), kv.at[i, 1 - side],
+              lambda dx, dj: kv_in.at[i, 2 * ((QT - dj) % QT) + dx])
+
+    enter_kv(0)
+
+    @pl.when(has_next)
+    def _():
+        @pl.loop(0, mine)
+        def _(i):
+            for a, ref in enumerate((k_ref, v_ref)):
+                send(ref.at[:, columns(first_head(side, seat) + i)], kv.at[i, 3 - side, a, seat],
+                     next_send.at[i, 1 - side], next_in.at[i, 1 - side], nxt)
+
+    def enter_qg(i):
+        enter(i, (q_ref, g_ref), qg.at[i, side], lambda dx, dj: qg_in.at[i])
+
+    if most > 1:
+        enter_kv(1)
 
     lane = lax.broadcasted_iota(jnp.int32, (1, QB), 1)
     for x in range(2):
@@ -136,12 +153,15 @@
             g_in[i] = jnp.zeros(g_in.shape[1:], BF)
 
     def own(i):
-        wait_for(kv.at[i, 0:2], kv_in.at[i])
-
-        @pl.when(has_next)
-        def _():
-            for s in range(2):
-                send(kv.at[i, s], kv.at[i, 2 + s], next_send.at[i, s], next_in.at[i, s], nxt)
+        for dx, dj in arrivals:
+            other, tile = peer(dx, dj)
+            s = 1 - other
+            for_tile = kv.at[i, s, :, tile]
+            wait_for(for_tile, kv_in.at[i, 2 * dj + dx])
+            if dx or dj:
+                @pl.when(has_next)
+                def _():
+                    send(for_tile, kv.at[i, 2 + s, :, tile], next_send.at[i, s], next_in.at[i, s], nxt)
 
     def leave(i, x, a):
         ref = (o_ref, dq_ref, dk_ref, dv_ref)[a]
@@ -247,6 +267,19 @@
                 leave(i, 1 - s, 2 + a)
 
     own(0)
+    enter_qg(0)
+
+    @pl.when(1 < mine)
+    def _():
+        own(1)
+
+    @pl.loop(1, most)
+    def _(i):
+        @pl.when(i + 1 < most)
+        def _():
+            enter_kv(i + 1)
+
+        enter_qg(i)
 
     @pl.loop(0, 2 * most + 2)
     def _(u):
@@ -274,9 +307,9 @@
                         send(g_out.at[i, s, a], g_in.at[i, s, a], g_send.at[i, s, a],
                              g_recv.at[i, s, a], prv)
 
-        @pl.when((odd == 0) & (i + 1 < mine))
-        def _():
-            own(i + 1)
+        @pl.when((odd == 0) & (i + 2 < mine))
+        def _():
+            own(i + 2)
 
         @pl.when((odd == 1) & (i >= 1) & (i < mine + 1))
         def _():
@@ -336,7 +369,7 @@
         pltpu.VMEM((most, 2, 2) + blocks, BF),
         pltpu.VMEM((most, 2, 2) + blocks, BF),
         pltpu.VMEM((most, 2, 4) + blocks, BF),
-        dma((most, 8)), dma((most,)), dma((most,)),
+        dma((most, 8)), dma((most, 8)), dma((most,)),
         dma((most, 2)), dma((most, 2)),
         dma((most, 2, 2)), dma((most, 2, 2)),
         dma((most, 2, 4, QT)), dma((4,)),
@@ -345,9 +378,9 @@
     anywhere = pl.BlockSpec(memory_space=pl.ANY)
     return pl.pallas_call(
         functools.partial(kernel, n, chip_heads),
-        out_shape=[jax.ShapeDtypeStruct((rows, width), BF)] * 4,
+        out_shape=[pltpu.VMEM((rows, width), BF)] * 4,
         in_specs=[smem, smem] + [anywhere] * 4,
-        out_specs=[anywhere] * 4,
+        out_specs=[pl.BlockSpec(memory_space=pltpu.VMEM)] * 4,
         scratch_shapes=scratch,
         compiler_params=pltpu.CompilerParams(
             collective_id=0, has_side_effects=True, vmem_limit_bytes=56 * 1024 * 1024

time: 102 us -> 93.7 us (0.919); the launches traced: 100 us -> 93.6 us
  Pallas kernels: 94.1 us -> 89.6 us
  local copies, waits for them, and re-layouts: 5.52 us -> 3.35 us
    pallas_call x1, Pallas kernels: 94.1 us -> 89.6 us  [shards(): pl.pallas_call(functools.partial(kernel, n, chip_heads), out_shape=[pltpu...]
    unnamed x10 -> x4, local copies, waits for them, and re-layouts: 5.52 us -> 3.35 us
where the time goes in v3:
time: 93.7 us; the launch traced here: 93.6 us
  Pallas kernels  89.6 us (96%)
  local copies, waits for them, and re-layouts  3.35 us (4%)
    pallas_call x1, Pallas kernels, shards(): pl.pallas_call(functools.partial(kernel, n, chip_heads), out_shape=[pltpu...  89.6 us
    unnamed x4, local copies, waits for them, and re-layouts  3.35 us

profile of v3, /device:TPU:17, one launch (start us, length us, event | category | flops | bytes accessed | tf_op | source)
XLA Modules:
  0.0 93.6 jit_solution(2632880043757940731)
XLA Ops:
  0.6 89.6 %shard_map.93 = (bf16[128,2560]{1,0:T(8,128)(2,1)S(1)}, bf16[128,2560]{1,0:T(8,128)(2,1)S(1)}, bf16[128,2560]{1,0:T(8,128)(2,1)S(1)}, bf16[128,2560]{1,0:T(8,128)(2,1)S(1)}) custom-call(s32[3,4,3]{2,1,0:T(4,128)} %pat_ref.1, s32[64]{0:T(128)} %win_ref.1, bf16[128,2560]{1,0:T(8,128)(2,1)} %q_ref.1, bf16[128,2560]{1,0:T(8,128)(2,1)} %k_ref.1, ...), custom_call_target="tpu_custom_call" | custom-call | tf_op jit(solution)/shard_map/pallas_call | solution.py:379
  90.2 0.8 copy.14
  91.1 0.8 copy.15
  91.9 0.8 copy.16
  92.7 0.8 copy.17

commit v4 on v2

v4 whole, which is shorter than its diff:
```python
import functools
import math

import jax
import jax.numpy as jnp
from jax import lax
from jax.experimental import pallas as pl
from jax.experimental.pallas import tpu as pltpu
from jax.sharding import PartitionSpec as P

HD = 128
TILE = 128
QT = 4
SEL = 3
W = 3
QH = 2
QB = QT // QH * TILE
NEG = -1e30
SCALE = 1.0 / math.sqrt(HD)
FACTOR = SCALE / math.log(2.0)
MESH = pl.DeviceIdType.MESH
BF = jnp.bfloat16
F32 = jnp.float32


def kernel(
    n,
    pat_ref, win_ref, q_ref, k_ref, v_ref, g_ref,
    o_ref, dq_ref, dk_ref, dv_ref,
    qg, kv, bias, kt, vt, score, pt, dst, gs, acc, g_out, g_in, outb,
    full_send, half_send, kv_in, qg_in, next_send, next_in, g_send, g_recv, out_send, out_recv,
):
    f = lax.axis_index("tm")
    seat = lax.axis_index("head")
    half = n // 2
    rows = n // 4
    row, x = f // 4, lax.rem(f, 4)
    pair, core = x // 2, lax.rem(seat, 2)
    upper = f // half
    full_heads = 4 * QT

    def column_of(at):
        return lax.rem(at // 2 + upper, 2)

    def full_head(other, at):
        return other * 4 + column_of(at) * 2 + lax.rem(at, 2)

    def half_at(e, p):
        return e % 2 + p * (3 - 2 * (e % 2)), 2 * lax.rem(e // 2 + upper, 2)

    my_head = (full_head(x, seat), full_heads + lax.rem(x + pair, 2) + 2 * column_of(seat))

    def device(frame):
        turn = (frame + n) // half - (f + n) // half
        return (frame, lax.rem(seat + 2 * turn + 2 * QT, QT))

    nxt = (device(f + 4), device(4 * (row + pair) + 3 - x))
    prv = (device(f - 4), device(4 * (row + pair - 1) + 3 - x))
    has_next = (row < rows - 1, 2 * row + pair < 2 * rows - 1)
    has_prev = (row > 0, 2 * row + pair > 0)

    def each_job(job, action):
        for at in range(2):
            @pl.when(job == at)
            def _():
                action(at)

    barrier = pltpu.get_barrier_semaphore()

    def greet(who):
        pl.semaphore_signal(barrier, inc=1, device_id=who, device_id_type=MESH)

    for dx in range(4):
        for dj in range(QT):
            if dx or dj:
                greet((4 * row + lax.rem(x + dx, 4), lax.rem(seat + dj, QT)))

    @pl.when(has_next[0])
    def _():
        greet(nxt[0])

    @pl.when(has_prev[0])
    def _():
        greet(prv[0])

    @pl.when((pair == 1) & has_next[0])
    def _():
        greet(nxt[1])

    @pl.when((pair == 0) & has_prev[0])
    def _():
        greet(prv[1])

    not_first = (row + rows - 1) // rows
    not_last = (2 * rows - 2 - row) // rows
    pl.semaphore_wait(barrier, 15 + (2 - pair) * not_first + (1 + pair) * not_last)

    def columns(head):
        return pl.ds(pl.multiple_of(head * HD, HD), HD)

    def wait_for(ref, sem):
        pltpu.make_async_copy(ref, ref, sem).wait()

    def send(src, dst, ssem, rsem, device):
        pltpu.make_async_remote_copy(
            src_ref=src, dst_ref=dst, send_sem=ssem, recv_sem=rsem,
            device_id=device, device_id_type=MESH,
        ).start()

    def place(refs, head, slot, ssem, rsem, other, at, local):
        cols = columns(head)
        if local is not False:
            @pl.when(local)
            def _():
                for a, ref in enumerate(refs):
                    pltpu.make_async_copy(ref.at[:, cols], slot.at[a, seat], rsem).start()

        @pl.when(True if local is False else jnp.logical_not(local))
        def _():
            for a, ref in enumerate(refs):
                send(ref.at[:, cols], slot.at[a, seat], ssem, rsem, (4 * row + other, at))

    side = lax.rem(x, 2)

    def enter_full(refs, slot, rsem, parity):
        for dx in (2, 1, 3, 0):
            for at in (parity, parity + 2):
                other = lax.rem(x + dx, 4)
                place(refs, full_head(other, at), slot, full_send.at[dx, at], rsem,
                      other, at, False if dx else seat == at)

    def enter_half(refs, slot, rsem):
        for e in range(4):
            other, at = half_at(e, pair)
            place(refs, full_heads + e, slot, half_send.at[e], rsem,
                  other, at, (other == x) & (at == seat))

    keys, tops = (k_ref, v_ref), (q_ref, g_ref)

    def full_kv(parity):
        enter_full(keys, kv.at[0, 3 - x], kv_in.at[0, 3 - x], parity)

    def full_qg(parity):
        enter_full(tops, qg.at[0, x], qg_in.at[0, x], parity)

    def own(job):
        for s in range(4 - 2 * job):
            wait_for(kv.at[job, s], kv_in.at[job, s])
            if s < 2:
                @pl.when(has_next[job])
                def _():
                    send(kv.at[job, s], kv.at[job, 4 - 2 * job + s],
                         next_send.at[job, s], next_in.at[job, s], nxt[job])

    full_kv(0)
    full_qg(0)
    enter_half(keys, kv.at[1, 1 - side], kv_in.at[1, 1 - side])

    lane = lax.broadcasted_iota(jnp.int32, (1, QB), 1)

    @pl.loop(0, 4)
    def _(fx):
        frame = 4 * row + fx
        limit = win_ref[frame]
        for h in range(QH):
            for lag in range(W):
                for t in range(QT):
                    both = []
                    for tile in (2 * h, 2 * h + 1):
                        hit = pat_ref[lag, tile, 0] == t
                        for s in range(1, SEL):
                            hit = hit | (pat_ref[lag, tile, s] == t)
                        hit = hit & (lag <= frame) & (lag < limit)
                        both.append(jnp.where(hit, 0.0, NEG).astype(F32))
                    bias[fx, h, lag * QT + t] = jnp.where(lane < TILE, both[0], both[1])

    full_kv(1)

    @pl.loop(0, 2)
    def _(job):
        @pl.loop(0, 6)
        def _(s):
            acc[job, s] = jnp.zeros(acc.shape[2:], F32)

    for job in range(2):
        for s in range(2):
            @pl.when(jnp.logical_not(has_prev[job]))
            def _():
                kv[job, 4 - 2 * job + s] = jnp.zeros(kv.shape[2:], BF)

            @pl.when(jnp.logical_not(has_next[job]))
            def _():
                g_in[job, s] = jnp.zeros(g_in.shape[2:], BF)

    @pl.when(core == 0)
    def _():
        own(0)

    full_qg(1)
    enter_half(tops, qg.at[1, side], qg_in.at[1, side])

    @pl.when(core == 1)
    def _():
        own(0)

    def leave(job, fr, a):
        ref = (o_ref, dq_ref, dk_ref, dv_ref)[a]
        where_to = ref.at[:, columns(jnp.where(job == 0, my_head[0], my_head[1]))]
        owner = fr + 2 * pair * job
        for dj in range(QT):
            at = lax.rem(seat + dj, QT)
            src = outb.at[job, fr, a, at]
            if dj:
                send(src, where_to, out_send.at[job, fr, a, dj], out_recv.at[a], (4 * row + owner, at))
            else:
                @pl.when(owner == x)
                def _():
                    pltpu.make_async_copy(src, where_to, out_recv.at[a]).start()

                @pl.when(owner != x)
                def _():
                    send(src, where_to, out_send.at[job, fr, a, dj], out_recv.at[a], (4 * row + owner, at))

    def nt(a, b):
        return lax.dot_general(a, b, (((1,), (1,)), ((), ())), preferred_element_type=F32)

    def mm(a, b):
        return jnp.dot(a, b, preferred_element_type=F32)

    def fold(block, op):
        return op(block.reshape(TILE // 8, 8, QB), axis=0)

    def attend(i, fr, base, x):

        def turn(slot):
            kt[slot] = kv[i, slot, 0].reshape(QT * TILE, HD).T
            vt[slot] = kv[i, slot, 1].reshape(QT * TILE, HD).T

        @pl.when(base == 0)
        def _():
            turn(0)
            turn(1)

        turn(base + 2)

        for h in range(QH):
            lanes = slice(h * QB, (h + 1) * QB)
            qh = qg[i, fr, 0, 2 * h:2 * h + 2].reshape(QB, HD)
            gh = qg[i, fr, 1, 2 * h:2 * h + 2].reshape(QB, HD)
            top = None
            for lag in range(W):
                for t in range(QT):
                    r = lag * QT + t
                    s = nt(kv[i, base + lag, 0, t], qh)
                    score[h, r] = s
                    here = fold(s, jnp.max) + bias[x, h, r]
                    top = here if top is None else jnp.maximum(top, here)
            top = jnp.max(top, axis=0, keepdims=True)
            total = None
            for r in range(W * QT):
                e = jnp.exp2(score[h, r] * FACTOR + (bias[x, h, r] - top) * FACTOR)
                pt[r, :, lanes] = e.astype(BF)
                here = fold(e, jnp.sum)
                total = here if total is None else total + here
            inverse = 1.0 / jnp.sum(total, axis=0, keepdims=True)
            out = None
            for lag in range(W):
                probs = pt[lag * QT:(lag + 1) * QT, :, lanes].reshape(QT * TILE, QB)
                here = mm(vt[base + lag], probs)
                out = here if out is None else out + here
            out = out * inverse
            scaled = (gh.T.astype(F32) * inverse).astype(BF)
            delta = jnp.sum(scaled.astype(F32) * out, axis=0, keepdims=True)
            outb[i, fr, 0, 2 * h:2 * h + 2] = out.astype(BF).T.reshape(2, TILE, HD)
            back = scaled.T
            gs[lanes] = back
            for lag in range(W):
                for t in range(QT):
                    r = lag * QT + t
                    dp = nt(kv[i, base + lag, 1, t], back) - delta
                    dst[r, :, lanes] = dp.astype(BF) * pt[r, :, lanes]
            dq = None
            for lag in range(W):
                ds = dst[lag * QT:(lag + 1) * QT, :, lanes].reshape(QT * TILE, QB)
                here = mm(kt[base + lag], ds)
                dq = here if dq is None else dq + here
            outb[i, fr, 1, 2 * h:2 * h + 2] = (dq * SCALE).astype(BF).T.reshape(2, TILE, HD)

        rows = qg[i, fr, 0].reshape(QT * TILE, HD)
        for lag in range(W):
            block = dst[lag * QT:(lag + 1) * QT].reshape(QT * TILE, QT * TILE)
            acc[i, base + lag, 0] += (mm(block, rows) * SCALE).reshape(QT, TILE, HD)
            block = pt[lag * QT:(lag + 1) * QT].reshape(QT * TILE, QT * TILE)
            acc[i, base + lag, 1] += mm(block, gs[...]).reshape(QT, TILE, HD)

    def back(job):
        @pl.when(has_prev[job])
        def _():
            for s in range(2):
                for a in range(2):
                    g_out[job, s, a] = acc[job, 4 - 2 * job + s, a].astype(BF)
                    send(g_out.at[job, s, a], g_in.at[job, s, a], g_send.at[job, s, a],
                         g_recv.at[job, s, a], prv[job])

    def finish(job):
        for s in range(2):
            for a in range(2):
                @pl.when(has_next[job])
                def _():
                    wait_for(g_in.at[job, s, a], g_recv.at[job, s, a])

                fr = 3 - 2 * job - s
                outb[job, fr, 2 + a] = (acc[job, s, a] + g_in[job, s, a].astype(F32)).astype(BF)
                leave(job, fr, 2 + a)

    units = 6 - 2 * core

    @pl.loop(0, units)
    def _(u):
        job = u // 4
        base = u - 4 * job
        fr = 3 - u + 2 * job
        wait_for(qg.at[job, fr], qg_in.at[job, fr])

        def arrived(at):
            @pl.when(has_prev[at])
            def _():
                s = lax.rem(u, 2)
                wait_for(kv.at[at, 4 - 2 * at + s], next_in.at[at, s])

        @pl.when(u >= 2)
        def _():
            each_job(job, arrived)

        attend(job, fr, base, fr + 2 * pair * job)
        leave(job, fr, 0)
        leave(job, fr, 1)

        @pl.when((u == 1) & (core == 0))
        def _():
            own(1)

        @pl.when((u == 2) | (u == 3))
        def _():
            for a in range(2):
                outb[0, fr, 2 + a] = acc[0, u, a].astype(BF)
                leave(0, fr, 2 + a)

        @pl.when((u == 3) | (u == 5))
        def _():
            each_job(job, back)

    finish(0)

    @pl.when(core == 0)
    def _():
        finish(1)

    for at in range(QT):
        for dx in range(4):
            if dx:
                wait_for(qg.at[0, 0, 0], full_send.at[dx, at])
            else:
                @pl.when(at != seat)
                def _():
                    wait_for(qg.at[0, 0, 0], full_send.at[dx, at])

    for e in range(4):
        other, at = half_at(e, pair)

        @pl.when(jnp.logical_not((other == x) & (at == seat)))
        def _():
            wait_for(qg.at[0, 0, 0], half_send.at[e])

    @pl.loop(0, 2 - core)
    def _(job):
        @pl.loop(0, 4 - 2 * job)
        def _(fr):
            for a in range(4):
                for dj in range(QT):
                    if dj:
                        wait_for(outb.at[job, fr, a, dj], out_send.at[job, fr, a, dj])
                    else:
                        @pl.when(fr + 2 * pair * job != x)
                        def _():
                            wait_for(outb.at[job, fr, a, dj], out_send.at[job, fr, a, dj])

    def sent(job):
        for s in range(2):
            @pl.when(has_next[job])
            def _():
                wait_for(kv.at[job, s], next_send.at[job, s])

            @pl.when(has_prev[job])
            def _():
                for a in range(2):
                    wait_for(g_out.at[job, s, a], g_send.at[job, s, a])

    sent(0)

    @pl.when(core == 0)
    def _():
        sent(1)

    for a, ref in enumerate((o_ref, dq_ref, dk_ref, dv_ref)):
        wait_for(ref, out_recv.at[a])


def shards(n, query, keys, values, grad_out, tile_pattern, window):
    rows, width = query.shape
    blocks = (QT, TILE, HD)
    dma = pltpu.SemaphoreType.DMA
    scratch = [
        pltpu.VMEM((2, 4, 2) + blocks, BF),
        pltpu.VMEM((2, 6, 2) + blocks, BF),
        pltpu.VMEM((4, QH, W * QT, 1, QB), F32),
        pltpu.VMEM((6, HD, QT * TILE), BF),
        pltpu.VMEM((6, HD, QT * TILE), BF),
        pltpu.VMEM((QH, W * QT, TILE, QB), F32),
        pltpu.VMEM((W * QT, TILE, QT * TILE), BF),
        pltpu.VMEM((W * QT, TILE, QT * TILE), BF),
        pltpu.VMEM((QT * TILE, HD), BF),
        pltpu.VMEM((2, 6, 2) + blocks, F32),
        pltpu.VMEM((2, 2, 2) + blocks, BF),
        pltpu.VMEM((2, 2, 2) + blocks, BF),
        pltpu.VMEM((2, 4, 4) + blocks, BF),
        dma((4, QT)), dma((4,)), dma((2, 4)), dma((2, 4)),
        dma((2, 2)), dma((2, 2)),
        dma((2, 2, 2)), dma((2, 2, 2)),
        dma((2, 4, 4, QT)), dma((4,)),
    ]
    smem = pl.BlockSpec(memory_space=pltpu.SMEM)
    anywhere = pl.BlockSpec(memory_space=pl.ANY)
    return pl.pallas_call(
        functools.partial(kernel, n),
        out_shape=[pltpu.VMEM((rows, width), BF)] * 4,
        in_specs=[smem, smem] + [anywhere] * 4,
        out_specs=[pl.BlockSpec(memory_space=pltpu.VMEM)] * 4,
        scratch_shapes=scratch,
        compiler_params=pltpu.CompilerParams(
            collective_id=0, has_side_effects=True, vmem_limit_bytes=56 * 1024 * 1024
        ),
    )(tile_pattern, window, query, keys, values, grad_out)


def solution(mesh):
    rows = P(("tm", "head"), None)
    return jax.shard_map(
        functools.partial(shards, mesh.shape["tm"]),
        mesh=mesh,
        in_specs=(rows, rows, rows, rows, P(), P()),
        out_specs=(rows, rows, rows, rows),
        check_vma=False,
    )
```

time: 102 us -> 80.6 us (0.79); the launches traced: 100 us -> 80.4 us
  Pallas kernels: 94.1 us -> 76.4 us
  local copies, waits for them, and re-layouts: 5.52 us -> 3.35 us
    pallas_call x1, Pallas kernels: 94.1 us -> 76.4 us  [shards(): pl.pallas_call(functools.partial(kernel, n), out_shape=[pltpu.VMEM((rows,...]
    unnamed x10 -> x4, local copies, waits for them, and re-layouts: 5.52 us -> 3.35 us
where the time goes in v4:
time: 80.6 us; the launch traced here: 80.4 us
  Pallas kernels  76.4 us (95%)
  local copies, waits for them, and re-layouts  3.35 us (4%)
    pallas_call x1, Pallas kernels, shards(): pl.pallas_call(functools.partial(kernel, n), out_shape=[pltpu.VMEM((rows,...  76.4 us
    unnamed x4, local copies, waits for them, and re-layouts  3.35 us

profile of v4, /device:TPU:17, one launch (start us, length us, event | category | flops | bytes accessed | tf_op | source)
XLA Modules:
  0.0 80.4 jit_solution(7624853999486035692)
XLA Ops:
  0.6 76.4 %shard_map.93 = (bf16[128,2560]{1,0:T(8,128)(2,1)S(1)}, bf16[128,2560]{1,0:T(8,128)(2,1)S(1)}, bf16[128,2560]{1,0:T(8,128)(2,1)S(1)}, bf16[128,2560]{1,0:T(8,128)(2,1)S(1)}) custom-call(s32[3,4,3]{2,1,0:T(4,128)} %pat_ref.1, s32[64]{0:T(128)} %win_ref.1, bf16[128,2560]{1,0:T(8,128)(2,1)} %q_ref.1, bf16[128,2560]{1,0:T(8,128)(2,1)} %k_ref.1, ...), custom_call_target="tpu_custom_call" | custom-call | tf_op jit(solution)/shard_map/pallas_call | solution.py:434
  77.1 0.8 %copy.14 = bf16[128,2560]{1,0:T(8,128)(2,1)} copy(bf16[128,2560]{1,0:T(8,128)(2,1)S(1)} %get-tuple-element.4) | data formatting | bytes 1310720
  77.9 0.8 %copy.15 = bf16[128,2560]{1,0:T(8,128)(2,1)} copy(bf16[128,2560]{1,0:T(8,128)(2,1)S(1)} %get-tuple-element.5) | data formatting | bytes 1310720
  78.8 0.8 %copy.16 = bf16[128,2560]{1,0:T(8,128)(2,1)} copy(bf16[128,2560]{1,0:T(8,128)(2,1)S(1)} %get-tuple-element.6) | data formatting | bytes 1310720
  79.6 0.8 %copy.17 = bf16[128,2560]{1,0:T(8,128)(2,1)} copy(bf16[128,2560]{1,0:T(8,128)(2,1)S(1)} %get-tuple-element.7) | data formatting | bytes 1310720

commit v5 on v4

--- a/solution.py
+++ b/solution.py
@@ -230,18 +230,18 @@
     def fold(block, op):
         return op(block.reshape(TILE // 8, 8, QB), axis=0)
 
-    def attend(i, fr, base, x):
+    def attend(i, fr, base, x, first):
 
         def turn(slot):
             kt[slot] = kv[i, slot, 0].reshape(QT * TILE, HD).T
             vt[slot] = kv[i, slot, 1].reshape(QT * TILE, HD).T
 
-        @pl.when(base == 0)
-        def _():
-            turn(0)
-            turn(1)
-
-        turn(base + 2)
+        turn(base)
+
+        @pl.when(first)
+        def _():
+            turn(base + 1)
+            turn(base + 2)
 
         for h in range(QH):
             lanes = slice(h * QB, (h + 1) * QB)
@@ -249,9 +249,10 @@
             gh = qg[i, fr, 1, 2 * h:2 * h + 2].reshape(QB, HD)
             top = None
             for lag in range(W):
+                block = nt(kv[i, base + lag, 0].reshape(QT * TILE, HD), qh)
                 for t in range(QT):
                     r = lag * QT + t
-                    s = nt(kv[i, base + lag, 0, t], qh)
+                    s = block[t * TILE:(t + 1) * TILE]
                     score[h, r] = s
                     here = fold(s, jnp.max) + bias[x, h, r]
                     top = here if top is None else jnp.maximum(top, here)
@@ -275,9 +276,10 @@
             back = scaled.T
             gs[lanes] = back
             for lag in range(W):
+                block = nt(kv[i, base + lag, 1].reshape(QT * TILE, HD), back)
                 for t in range(QT):
                     r = lag * QT + t
-                    dp = nt(kv[i, base + lag, 1, t], back) - delta
+                    dp = block[t * TILE:(t + 1) * TILE] - delta
                     dst[r, :, lanes] = dp.astype(BF) * pt[r, :, lanes]
             dq = None
             for lag in range(W):
@@ -318,21 +320,21 @@
     @pl.loop(0, units)
     def _(u):
         job = u // 4
-        base = u - 4 * job
-        fr = 3 - u + 2 * job
+        fr = u - 4 * job
+        base = 3 - 2 * job - fr
         wait_for(qg.at[job, fr], qg_in.at[job, fr])
 
         def arrived(at):
             @pl.when(has_prev[at])
             def _():
-                s = lax.rem(u, 2)
-                wait_for(kv.at[at, 4 - 2 * at + s], next_in.at[at, s])
-
-        @pl.when(u >= 2)
+                for s in range(2):
+                    wait_for(kv.at[at, 4 - 2 * at + s], next_in.at[at, s])
+
+        @pl.when((u == 0) | (u == 4))
         def _():
             each_job(job, arrived)
 
-        attend(job, fr, base, fr + 2 * pair * job)
+        attend(job, fr, base, fr + 2 * pair * job, (u == 0) | (u == 4))
         leave(job, fr, 0)
         leave(job, fr, 1)
 
@@ -340,17 +342,19 @@
         def _():
             own(1)
 
+        @pl.when((u == 1) | (u == 5))
+        def _():
+            each_job(job, back)
+
         @pl.when((u == 2) | (u == 3))
         def _():
             for a in range(2):
-                outb[0, fr, 2 + a] = acc[0, u, a].astype(BF)
-                leave(0, fr, 2 + a)
-
-        @pl.when((u == 3) | (u == 5))
-        def _():
-            each_job(job, back)
-
-    finish(0)
+                outb[0, u - 2, 2 + a] = acc[0, 5 - u, a].astype(BF)
+                leave(0, u - 2, 2 + a)
+
+        @pl.when(u == 3)
+        def _():
+            finish(0)
 
     @pl.when(core == 0)
     def _():
@@ -404,6 +408,15 @@
 
     for a, ref in enumerate((o_ref, dq_ref, dk_ref, dv_ref)):
         wait_for(ref, out_recv.at[a])
+
+
+def put(*refs):
+    sems = refs[8]
+    copies = [pltpu.make_async_copy(refs[a], refs[4 + a], sems.at[a]) for a in range(4)]
+    for copy in copies:
+        copy.start()
+    for copy in copies:
+        copy.wait()
 
 
 def shards(n, query, keys, values, grad_out, tile_pattern, window):
@@ -431,7 +444,7 @@
     ]
     smem = pl.BlockSpec(memory_space=pltpu.SMEM)
     anywhere = pl.BlockSpec(memory_space=pl.ANY)
-    return pl.pallas_call(
+    held = pl.pallas_call(
         functools.partial(kernel, n),
         out_shape=[pltpu.VMEM((rows, width), BF)] * 4,
         in_specs=[smem, smem] + [anywhere] * 4,
@@ -441,6 +454,13 @@
             collective_id=0, has_side_effects=True, vmem_limit_bytes=56 * 1024 * 1024
         ),
     )(tile_pattern, window, query, keys, values, grad_out)
+    return pl.pallas_call(
+        put,
+        out_shape=[jax.ShapeDtypeStruct((rows, width), BF)] * 4,
+        in_specs=[pl.BlockSpec(memory_space=pltpu.VMEM)] * 4,
+        out_specs=[anywhere] * 4,
+        scratch_shapes=[dma((4,))],
+    )(*[pltpu.with_memory_space_constraint(part, pltpu.VMEM) for part in held])
 
 
 def solution(mesh):

time: 80.6 us -> 77.7 us (0.964)
  the two profiles are of different devices: /device:TPU:17 before, /device:TPU:21 now
where the time goes in v5:
time: 77.7 us; the launch traced here: 77.6 us
  Pallas kernels  76.9 us (99%)
    pallas_call x1, Pallas kernels, shards(): pl.pallas_call(functools.partial(kernel, n), out_shape=[pltpu.VMEM((rows,...  75.4 us

profile of v5, /device:TPU:21, one launch (start us, length us, event | category | flops | bytes accessed | tf_op | source)
XLA Modules:
  0.0 77.6 jit_solution(11671313030863865900)
XLA Ops:
  0.6 75.4 %shard_map.93 = (bf16[128,2560]{1,0:T(8,128)(2,1)S(1)}, bf16[128,2560]{1,0:T(8,128)(2,1)S(1)}, bf16[128,2560]{1,0:T(8,128)(2,1)S(1)}, bf16[128,2560]{1,0:T(8,128)(2,1)S(1)}) custom-call(s32[3,4,3]{2,1,0:T(4,128)} %pat_ref.1, s32[64]{0:T(128)} %win_ref.1, bf16[128,2560]{1,0:T(8,128)(2,1)} %q_ref.1, bf16[128,2560]{1,0:T(8,128)(2,1)} %k_ref.1, ...), custom_call_target="tpu_custom_call" | custom-call | tf_op jit(solution)/shard_map/pallas_call | solution.py:447
  76.1 1.5 %shard_map.94 = (bf16[128,2560]{1,0:T(8,128)(2,1)}, bf16[128,2560]{1,0:T(8,128)(2,1)}, bf16[128,2560]{1,0:T(8,128)(2,1)}, bf16[128,2560]{1,0:T(8,128)(2,1)}) custom-call(bf16[128,2560]{1,0:T(8,128)(2,1)S(1)} %get-tuple-element.8.refs_0_, bf16[128,2560]{1,0:T(8,128)(2,1)S(1)} %get-tuple-element.9.refs_1_, bf16[128,2560]{1,0:T(8,128)(2,1)S(1)} %get-tuple-element.10.refs_2_, ...), custom_call_target="tpu_custom_call" | custom-call | tf_op jit(solution)/shard_map/pallas_call | solution.py:457

commit v6 on v5

--- a/solution.py
+++ b/solution.py
@@ -25,10 +25,11 @@
 
 def kernel(
     n,
-    pat_ref, win_ref, q_ref, k_ref, v_ref, g_ref,
+    pat_any, win_any, q_ref, k_ref, v_ref, g_ref,
     o_ref, dq_ref, dk_ref, dv_ref,
     qg, kv, bias, kt, vt, score, pt, dst, gs, acc, g_out, g_in, outb,
     full_send, half_send, kv_in, qg_in, next_send, next_in, g_send, g_recv, out_send, out_recv,
+    pat_ref, win_ref, table_in,
 ):
     f = lax.axis_index("tm")
     seat = lax.axis_index("head")
@@ -65,6 +66,11 @@
             def _():
                 action(at)
 
+    tables = [pltpu.make_async_copy(pat_any, pat_ref, table_in.at[0]),
+              pltpu.make_async_copy(win_any, win_ref, table_in.at[1])]
+    for table in tables:
+        table.start()
+
     barrier = pltpu.get_barrier_semaphore()
 
     def greet(who):
@@ -157,6 +163,8 @@
     enter_half(keys, kv.at[1, 1 - side], kv_in.at[1, 1 - side])
 
     lane = lax.broadcasted_iota(jnp.int32, (1, QB), 1)
+    for table in tables:
+        table.wait()
 
     @pl.loop(0, 4)
     def _(fx):
@@ -338,7 +346,7 @@
         leave(job, fr, 0)
         leave(job, fr, 1)
 
-        @pl.when((u == 1) & (core == 0))
+        @pl.when((u == 0) & (core == 0))
         def _():
             own(1)
 
@@ -441,13 +449,13 @@
         dma((2, 2)), dma((2, 2)),
         dma((2, 2, 2)), dma((2, 2, 2)),
         dma((2, 4, 4, QT)), dma((4,)),
+        pltpu.SMEM(tile_pattern.shape, jnp.int32), pltpu.SMEM(window.shape, jnp.int32), dma((2,)),
     ]
-    smem = pl.BlockSpec(memory_space=pltpu.SMEM)
     anywhere = pl.BlockSpec(memory_space=pl.ANY)
     held = pl.pallas_call(
         functools.partial(kernel, n),
         out_shape=[pltpu.VMEM((rows, width), BF)] * 4,
-        in_specs=[smem, smem] + [anywhere] * 4,
+        in_specs=[anywhere] * 6,
         out_specs=[pl.BlockSpec(memory_space=pltpu.VMEM)] * 4,
         scratch_shapes=scratch,
         compiler_params=pltpu.CompilerParams(

time: 77.7 us -> 75.5 us (0.972)
  the two profiles are of different devices: /device:TPU:21 before, /device:TPU:17 now
where the time goes in v6:
time: 75.5 us; the launch traced here: 74.5 us
  Pallas kernels  73.8 us (98%)
    pallas_call x1, Pallas kernels, shards(): pl.pallas_call(functools.partial(kernel, n), out_shape=[pltpu.VMEM((rows,...  72.3 us
    pallas_call x1, Pallas kernels, shards(): pl.pallas_call(put, out_shape=[jax.ShapeDtypeStruct((rows, width), BF)] *...  1.52 us

profile of v6, /device:TPU:17, one launch (start us, length us, event | category | flops | bytes accessed | tf_op | source)
XLA Modules:
  0.0 74.5 jit_solution(17477748148610229443)
XLA Ops:
  0.6 72.3 %shard_map.93 = (bf16[128,2560]{1,0:T(8,128)(2,1)S(1)}, bf16[128,2560]{1,0:T(8,128)(2,1)S(1)}, bf16[128,2560]{1,0:T(8,128)(2,1)S(1)}, bf16[128,2560]{1,0:T(8,128)(2,1)S(1)}) custom-call(s32[3,4,3]{2,1,0:T(4,128)} %pat_any.1, s32[64]{0:T(128)} %win_any.1, bf16[128,2560]{1,0:T(8,128)(2,1)} %q_ref.1, bf16[128,2560]{1,0:T(8,128)(2,1)} %k_ref.1, ...), custom_call_target="tpu_custom_call" | custom-call | tf_op jit(solution)/shard_map/pallas_call | solution.py:455
  72.9 1.5 %shard_map.94 = (bf16[128,2560]{1,0:T(8,128)(2,1)}, bf16[128,2560]{1,0:T(8,128)(2,1)}, bf16[128,2560]{1,0:T(8,128)(2,1)}, bf16[128,2560]{1,0:T(8,128)(2,1)}) custom-call(bf16[128,2560]{1,0:T(8,128)(2,1)S(1)} %get-tuple-element.8.refs_0_, bf16[128,2560]{1,0:T(8,128)(2,1)S(1)} %get-tuple-element.9.refs_1_, bf16[128,2560]{1,0:T(8,128)(2,1)S(1)} %get-tuple-element.10.refs_2_, ...), custom_call_target="tpu_custom_call" | custom-call | tf_op jit(solution)/shard_map/pallas_call | solution.py:465

commit v7 on v6

--- a/solution.py
+++ b/solution.py
@@ -343,16 +343,17 @@
             each_job(job, arrived)
 
         attend(job, fr, base, fr + 2 * pair * job, (u == 0) | (u == 4))
+
+        @pl.when((u == 1) | (u == 5))
+        def _():
+            each_job(job, back)
+
         leave(job, fr, 0)
         leave(job, fr, 1)
 
         @pl.when((u == 0) & (core == 0))
         def _():
             own(1)
-
-        @pl.when((u == 1) | (u == 5))
-        def _():
-            each_job(job, back)
 
         @pl.when((u == 2) | (u == 3))
         def _():

time: 75.5 us -> 75.4 us (level)
  no operation moved by 1% of the time
where the time goes in v7:
time: 75.4 us; the launch traced here: 74.5 us
  Pallas kernels  73.8 us (98%)
    pallas_call x1, Pallas kernels, shards(): pl.pallas_call(functools.partial(kernel, n), out_shape=[pltpu.VMEM((rows,...  72.3 us
    pallas_call x1, Pallas kernels, shards(): pl.pallas_call(put, out_shape=[jax.ShapeDtypeStruct((rows, width), BF)] *...  1.52 us

profile of v7, /device:TPU:17, one launch (start us, length us, event | category | flops | bytes accessed | tf_op | source)
XLA Modules:
  0.0 74.5 jit_solution(13468564841337897253)
XLA Ops:
  0.6 72.3 %shard_map.93 = (bf16[128,2560]{1,0:T(8,128)(2,1)S(1)}, bf16[128,2560]{1,0:T(8,128)(2,1)S(1)}, bf16[128,2560]{1,0:T(8,128)(2,1)S(1)}, bf16[128,2560]{1,0:T(8,128)(2,1)S(1)}) custom-call(s32[3,4,3]{2,1,0:T(4,128)} %pat_any.1, s32[64]{0:T(128)} %win_any.1, bf16[128,2560]{1,0:T(8,128)(2,1)} %q_ref.1, bf16[128,2560]{1,0:T(8,128)(2,1)} %k_ref.1, ...), custom_call_target="tpu_custom_call" | custom-call | tf_op jit(solution)/shard_map/pallas_call | solution.py:456
  72.9 1.5 %shard_map.94 = (bf16[128,2560]{1,0:T(8,128)(2,1)}, bf16[128,2560]{1,0:T(8,128)(2,1)}, bf16[128,2560]{1,0:T(8,128)(2,1)}, bf16[128,2560]{1,0:T(8,128)(2,1)}) custom-call(bf16[128,2560]{1,0:T(8,128)(2,1)S(1)} %get-tuple-element.8.refs_0_, bf16[128,2560]{1,0:T(8,128)(2,1)S(1)} %get-tuple-element.9.refs_1_, bf16[128,2560]{1,0:T(8,128)(2,1)S(1)} %get-tuple-element.10.refs_2_, ...), custom_call_target="tpu_custom_call" | custom-call | tf_op jit(solution)/shard_map/pallas_call | solution.py:466
